TPU v7x, 512 devices: a whole 4x4x16 slice. The times are simulated.
512 devices in a mesh: expert: 64 (over y, z), tensor: 8 (over x, core).
Axes of the slice: x: 4, y: 4, z: 16, core: 2. Of those that a mesh axis runs over, the one named last changes fastest.
Arguments:
- tokens: bfloat16 [65536, 1024], P(('expert', 'tensor')), may hold values from -6 to 6
- out_grad: bfloat16 [65536, 1024], P(('expert', 'tensor')), may hold values from -6 to 6
- expert_ids: int32 [65536, 2], P(('expert', 'tensor')), may hold values from 0 to 63, all different within a row; in each aligned block of 128 rows (0 to 127, 128 to 255, ...) at most 5 rows name the same one
- gate_levels: int32 [65536, 2], P(('expert', 'tensor')), may hold values from 1 to 255
- gate_weight: bfloat16 [64, 1024, 2048], P('expert', None, 'tensor'), may hold values from -0.1875 to 0.1875
- up_weight: bfloat16 [64, 1024, 2048], P('expert', None, 'tensor'), may hold values from -0.1875 to 0.1875
- down_weight: bfloat16 [64, 1024, 2048], P('expert', None, 'tensor'), may hold values from -0.125 to 0.125
Outputs:
- token_grad: bfloat16 [65536, 1024], P(('expert', 'tensor'))
Inputs may be any that keep to these rules, and one draw needn't show every extreme that they name: `expert_ids`: A token's 2 experts differ. Among the 128 tokens of one device no expert is named more than 5 times, a bound that some block reaches.
All inputs are finite; a program needn't handle non-finite values.
Results may differ from a plain program's by a relative error of at most 0.01.
Values may be sent and summed in bfloat16 or wider, within the bound.
No kernel may reach another device: no remote copies, remote signals or barrier semaphores. Data moves between devices by JAX's collectives and lax.ppermute only.
A program may use at most 64 MiB of HBM per device.

v0:
```python
import jax
import jax.numpy as jnp
from jax import lax
from jax.sharding import PartitionSpec as P

level_scale = 1.0 / 256.0


def expert_grad(rows_in, grads_in, gate_cols, up_cols, down_cols):
    gate_pre = jnp.dot(rows_in, gate_cols, preferred_element_type=jnp.float32)
    up_pre = jnp.dot(rows_in, up_cols, preferred_element_type=jnp.float32)
    hidden_grad = jnp.dot(grads_in, down_cols, preferred_element_type=jnp.float32)
    sigmoid_val = jax.nn.sigmoid(gate_pre)
    up_grad = (hidden_grad * gate_pre * sigmoid_val).astype(jnp.bfloat16)
    gate_grad = (
        hidden_grad * up_pre * sigmoid_val * (1.0 + gate_pre * (1.0 - sigmoid_val))
    ).astype(jnp.bfloat16)
    joined_grad = jnp.concatenate([gate_grad, up_grad], axis=1)
    joined_cols = jnp.concatenate([gate_cols, up_cols], axis=1)
    back_dims = (((1,), (1,)), ((), ()))
    result = lax.dot_general(
        joined_grad, joined_cols, back_dims, preferred_element_type=jnp.float32
    )
    return result.astype(jnp.bfloat16)


def on_device(tokens, out_grad, expert_ids, gate_levels, gate_weight, up_weight, down_weight):
    tok_count, width = tokens.shape
    top_count = expert_ids.shape[1]
    experts = lax.axis_size("expert")
    capacity = max(2, 5 * tok_count * top_count // (4 * experts))
    slots = experts * capacity
    flat_ids = expert_ids.reshape(-1)
    lane_ids = jnp.arange(experts, dtype=jnp.int32)
    onehot = (flat_ids[:, None] == lane_ids[None, :]).astype(jnp.int32)
    slot_rank = jnp.sum(jnp.cumsum(onehot, axis=0) * onehot, axis=1) - 1
    slot_ids = flat_ids * capacity + slot_rank
    assign = (slot_ids[:, None] == jnp.arange(slots, dtype=jnp.int32)[None, :]).astype(jnp.float32)
    assign = assign.reshape(tok_count, top_count, slots)
    dispatch = jnp.sum(assign, axis=1).astype(jnp.bfloat16)
    route_scale = gate_levels.astype(jnp.float32) * level_scale
    combiner = jnp.sum(assign * route_scale[:, :, None], axis=1)
    send_dims = (((0,), (0,)), ((), ()))
    send_rows = lax.dot_general(
        dispatch, tokens, send_dims, preferred_element_type=jnp.float32
    ).astype(jnp.bfloat16)
    send_grads = lax.dot_general(
        dispatch, out_grad, send_dims, preferred_element_type=jnp.float32
    ).astype(jnp.bfloat16)
    packed = jnp.stack([send_rows, send_grads])
    received = lax.all_to_all(packed, "expert", split_axis=1, concat_axis=1, tiled=True)
    gate_cols = gate_weight[0]
    up_cols = up_weight[0]
    down_cols = down_weight[0]
    part_rows = lax.all_gather(received, "tensor", axis=1, tiled=True)
    partials = expert_grad(part_rows[0], part_rows[1], gate_cols, up_cols, down_cols)
    partials = partials.reshape(-1, slots, width)
    returned = lax.all_to_all(
        lax.all_to_all(partials, "expert", split_axis=1, concat_axis=1, tiled=True),
        "tensor",
        split_axis=0,
        concat_axis=0,
        tiled=True,
    )
    contrib = jnp.sum(returned.astype(jnp.float32), axis=0)
    token_grad = jnp.dot(
        combiner, contrib, precision=lax.Precision.HIGHEST, preferred_element_type=jnp.float32
    )
    return token_grad.astype(jnp.bfloat16)


def solution(mesh):
    return jax.shard_map(
        on_device,
        mesh=mesh,
        in_specs=(
            P(("expert", "tensor"), None),
            P(("expert", "tensor"), None),
            P(("expert", "tensor"), None),
            P(("expert", "tensor"), None),
            P("expert", None, "tensor"),
            P("expert", None, "tensor"),
            P("expert", None, "tensor"),
        ),
        out_specs=P(("expert", "tensor"), None),
        check_vma=False,
    )
```

profile of v0, /device:TPU:1, one launch (start us, length us, event | category | flops | bytes accessed | tf_op | source)
XLA Modules:
  0.0 501.7 jit_solution(4049381263710705938)
XLA Ops:
  6.5 0.0 copy-start
  6.5 0.0 all-gather.2.cloned.1.call-start
  6.5 0.8 copy.53
  7.4 0.1 eq.39
  7.5 0.1 eq.43
  7.7 0.6 reduce-window.6
  8.3 0.2 slice_reduce_fusion
  8.5 0.1 fusion.17
  8.6 0.1 sub.10
  8.8 0.1 copy.56
  8.8 0.7 multiply_add_fusion
  9.6 0.7 convert_multiply_fusion
  10.2 0.1 convert_reduce_fusion.1
  10.3 1.3 fusion.11
  11.6 1.3 fusion.10
  12.9 0.1 pad_maximum_fusion
  13.0 1.3 copy.57
  14.3 79.5 %all_to_all.15 = bf16[2,320,1024]{2,0,1:T(2,128)(2,1)S(1)} all-to-all(bf16[2,320,1024]{2,0,1:T(2,128)(2,1)S(1)} %copy.57), channel_id=1, replica_groups=mesh['expert'=64,'tensor'=8] {'expert'}, dimensions={1} | all-to-all | bytes 2621440 | tf_op jit(solution)/shard_map/all_to_all | solution.py:51
  93.9 0.0 copy-start.2
  93.9 1.4 copy.58
  95.3 0.0 all-gather.2.cloned.1.call-update
  95.3 64.1 %all-gather.2.cloned.1.call-done = bf16[2,2560,1024]{2,1,0:T(8,128)(2,1)} async-done(((bf16[2,320,1024]{2,1,0:T(8,128)(2,1)}), bf16[2,2560,1024]{2,1,0:T(8,128)(2,1)}) %all-gather.2.cloned.1.call-update) | async-done | bytes 10485776 | tf_op jit(solution)/shard_map/all_gather | solution.py:55
  159.4 0.0 copy-done.2
  159.5 0.0 copy-start.1
  159.5 4.2 fusion.1
  163.7 0.0 copy-done
  163.7 1.3 copy-done.1
  165.0 0.0 copy-start.3
  165.0 2.2 multiply_convert_fusion
  167.2 0.0 copy-done.3
  167.2 2.6 fusion.6
  169.7 3.2 convolution_convert_fusion
  173.0 2.9 copy.59
  175.9 245.5 %all_to_all.16 = bf16[8,320,1024]{2,0,1:T(8,128)(2,1)S(1)} all-to-all(bf16[8,320,1024]{2,0,1:T(8,128)(2,1)S(1)} %copy.59), channel_id=1, replica_groups=mesh['expert'=64,'tensor'=8] {'expert'}, dimensions={1} | all-to-all | bytes 10485760 | tf_op jit(solution)/shard_map/all_to_all | solution.py:59
  421.3 2.9 copy.60
  424.2 67.6 %all_to_all.17 = bf16[8,320,1024]{2,1,0:T(8,128)(2,1)S(1)} all-to-all(bf16[8,320,1024]{2,1,0:T(8,128)(2,1)S(1)} %copy.60), channel_id=1, replica_groups=mesh['expert'=64,'tensor'=8] {'tensor'}, dimensions={0} | all-to-all | bytes 10485760 | tf_op jit(solution)/shard_map/all_to_all | solution.py:58
  491.9 1.2 convert_reduce_fusion
  493.0 1.8 convolution_convert_fusion.3
  (4 shorter events, 0.1 us)
Async XLA Ops:
  6.5 157.2 %copy-start = (bf16[1,1024,256]{2,1,0:T(8,128)(2,1)S(1)}, bf16[1,1024,256]{2,1,0:T(8,128)(2,1)}, u32[]{:S(2)}) copy-start(bf16[1,1024,256]{2,1,0:T(8,128)(2,1)} %param.13) | copy-start | bytes 1572868
  6.5 152.9 %all-gather.2.cloned.1.call-start = ((), (), s32[]{:S(2)}) async-start(), calls=%async_computation.3 | async-start | bytes 11796480 | tf_op jit(solution)/shard_map/all_gather | solution.py:55
  93.9 65.6 %copy-start.2 = (bf16[1,1024,256]{2,1,0:T(8,128)(2,1)S(1)}, bf16[1,1024,256]{2,1,0:T(8,128)(2,1)}, u32[]{:S(2)}) copy-start(bf16[1,1024,256]{2,1,0:T(8,128)(2,1)} %param.11) | copy-start | bytes 1572868
  159.5 5.5 %copy-start.1 = (bf16[2,2560,1024]{2,1,0:T(8,128)(2,1)S(1)}, bf16[2,2560,1024]{2,1,0:T(8,128)(2,1)}, u32[]{:S(2)}) copy-start(bf16[2,2560,1024]{2,1,0:T(8,128)(2,1)} %all-gather.2.cloned.1.call-done) | copy-start | bytes 31457284
  165.0 2.2 copy-start.3
Sparse Core Ops, SparseCore 0:
  95.4 63.9 all-gather.1
where the time goes:
time: 502 us
  blocking collectives  393 us (78%)
  waiting for transfers between devices  64.2 us (13%)
  matrix products  16.5 us (3%)
  between operations  13.5 us (3%)
  local copies, waits for them, and re-layouts  11.4 us (2%)
    all_to_all x1, blocking collectives, on_device(): lax.all_to_all(partials, 'expert', split_axis=1, concat_axis=1, tiled=True)  245 us
    all_to_all x1, blocking collectives, on_device(): lax.all_to_all(packed, 'expert', split_axis=1, concat_axis=1, tiled=True)  79.5 us
    all_to_all x1, blocking collectives, on_device(): lax.all_to_all(lax.all_to_all(partials, 'expert', split_axis=1, concat_ax...  67.6 us
    all_gather x1, waiting for transfers between devices, on_device(): part_rows = lax.all_gather(received, 'tensor', axis=1, tiled=True)  64.1 us
  transfers between devices with their start and end apart: 1, of which 1 were waited for; matrix products, arithmetic and copies ran while one was open for 0% of the time, Pallas kernels for 0%

commit v1 on v0

v1 whole, which is shorter than its diff:
```python
import jax
import jax.numpy as jnp
from jax import lax
from jax.experimental import pallas as pl
from jax.experimental.pallas import tpu as pltpu
from jax.sharding import PartitionSpec as P

level_scale = 1.0 / 256.0
vmem_limit = 56 * 1024 * 1024


def route_kernel(capacity, experts, tok_ref, grad_ref, ids_ref, lev_ref, send_ref, comb_ref):
    count = ids_ref.shape[1]
    slots = comb_ref.shape[0]
    ids0 = ids_ref[0:1, :]
    ids1 = ids_ref[1:2, :]
    lane_e = lax.broadcasted_iota(jnp.int32, (experts, count), 0)
    hot0 = (lane_e == ids0).astype(jnp.float32)
    hot1 = (lane_e == ids1).astype(jnp.float32)
    row_i = lax.broadcasted_iota(jnp.int32, (count, count), 0)
    col_i = lax.broadcasted_iota(jnp.int32, (count, count), 1)
    upper = (row_i <= col_i).astype(jnp.bfloat16)
    run0 = jnp.dot(hot0.astype(jnp.bfloat16), upper, preferred_element_type=jnp.float32)
    run1 = jnp.dot(hot1.astype(jnp.bfloat16), upper, preferred_element_type=jnp.float32)
    run1 = run1 + jnp.sum(hot0, axis=1, keepdims=True)
    rank0 = jnp.sum(hot0 * run0, axis=0, keepdims=True).astype(jnp.int32) - 1
    rank1 = jnp.sum(hot1 * run1, axis=0, keepdims=True).astype(jnp.int32) - 1
    slot0 = ids0 * capacity + rank0
    slot1 = ids1 * capacity + rank1
    slot_i = lax.broadcasted_iota(jnp.int32, (slots, count), 0)
    at0 = slot_i == slot0
    at1 = slot_i == slot1
    scale = lev_ref[...].astype(jnp.float32) * level_scale
    comb = jnp.where(at0, scale[0:1, :], 0.0) + jnp.where(at1, scale[1:2, :], 0.0)
    comb_ref[...] = comb.astype(jnp.bfloat16)
    pick = jnp.where(at0 | at1, 1.0, 0.0).astype(jnp.bfloat16)
    send_ref[0] = jnp.dot(pick, tok_ref[...], preferred_element_type=jnp.float32).astype(jnp.bfloat16)
    send_ref[1] = jnp.dot(pick, grad_ref[...], preferred_element_type=jnp.float32).astype(jnp.bfloat16)


def expert_kernel(rows_ref, gate_ref, up_ref, down_ref, out_ref, acc_ref):
    block = pl.program_id(0)
    rows = rows_ref[0]
    grads = rows_ref[1]
    gate_pre = jnp.dot(rows, gate_ref[0], preferred_element_type=jnp.float32)
    up_pre = jnp.dot(rows, up_ref[0], preferred_element_type=jnp.float32)
    hidden_grad = jnp.dot(grads, down_ref[0], preferred_element_type=jnp.float32)
    sig = jax.nn.sigmoid(gate_pre)
    up_grad = (hidden_grad * gate_pre * sig).astype(jnp.bfloat16)
    gate_grad = (hidden_grad * up_pre * sig * (1.0 + gate_pre * (1.0 - sig))).astype(jnp.bfloat16)
    back = (((1,), (1,)), ((), ()))
    part = lax.dot_general(gate_grad, gate_ref[0], back, preferred_element_type=jnp.float32)
    part = part + lax.dot_general(up_grad, up_ref[0], back, preferred_element_type=jnp.float32)

    @pl.when(block == 0)
    def _():
        acc_ref[...] = part

    @pl.when(block > 0)
    def _():
        acc_ref[...] = acc_ref[...] + part

    @pl.when(block == pl.num_programs(0) - 1)
    def _():
        out_ref[...] = acc_ref[...].astype(jnp.bfloat16)


def on_device(tokens, out_grad, expert_ids, gate_levels, gate_weight, up_weight, down_weight):
    tok_count, width = tokens.shape
    experts = lax.axis_size("expert")
    tensor = lax.axis_size("tensor")
    capacity = 5
    slots = experts * capacity
    cols = gate_weight.shape[2]
    gate_all = lax.all_gather(gate_weight, "tensor", axis=0, tiled=True)
    up_all = lax.all_gather(up_weight, "tensor", axis=0, tiled=True)
    down_all = lax.all_gather(down_weight, "tensor", axis=0, tiled=True)
    vmem = pl.BlockSpec(memory_space=pltpu.VMEM)
    send, comb = pl.pallas_call(
        lambda *refs: route_kernel(capacity, experts, *refs),
        name="route",
        out_shape=(
            jax.ShapeDtypeStruct((2, slots, width), jnp.bfloat16),
            jax.ShapeDtypeStruct((slots, tok_count), jnp.bfloat16),
        ),
        in_specs=[vmem] * 4,
        out_specs=(vmem, vmem),
    )(tokens, out_grad, expert_ids.T, gate_levels.T)
    received = lax.all_to_all(send, "expert", split_axis=1, concat_axis=1, tiled=True)
    weight_spec = pl.BlockSpec((1, width, cols), lambda b: (b, 0, 0))
    result = pl.pallas_call(
        expert_kernel,
        name="expert_grad",
        grid=(tensor,),
        out_shape=jax.ShapeDtypeStruct((slots, width), jnp.bfloat16),
        in_specs=[pl.BlockSpec((2, slots, width), lambda b: (0, 0, 0)), weight_spec, weight_spec, weight_spec],
        out_specs=pl.BlockSpec((slots, width), lambda b: (0, 0)),
        scratch_shapes=[pltpu.VMEM((slots, width), jnp.float32)],
        compiler_params=pltpu.CompilerParams(vmem_limit_bytes=vmem_limit),
    )(received, gate_all, up_all, down_all)
    lanes = width // 8
    returned = lax.all_to_all(result.reshape(slots, 8, lanes), "expert", split_axis=0, concat_axis=0, tiled=True)
    returned = returned.reshape(slots, width)
    total = lax.dot_general(comb, returned, (((0,), (0,)), ((), ())), preferred_element_type=jnp.float32)
    return total.astype(jnp.bfloat16)


def solution(mesh):
    return jax.shard_map(
        on_device,
        mesh=mesh,
        in_specs=(
            P(("expert", "tensor"), None),
            P(("expert", "tensor"), None),
            P(("expert", "tensor"), None),
            P(("expert", "tensor"), None),
            P("expert", None, "tensor"),
            P("expert", None, "tensor"),
            P("expert", None, "tensor"),
        ),
        out_specs=P(("expert", "tensor"), None),
        check_vma=False,
    )
```

time: 502 us -> 218 us (0.43)
  blocking collectives: 393 us -> 130 us
  Pallas kernels: 0 us -> 20.7 us
  waiting for transfers between devices: 64.2 us -> 45.6 us
  matrix products: 16.5 us -> 1.03 us
  local copies, waits for them, and re-layouts: 11.4 us -> 5.38 us
    all_to_all x3 -> x2, blocking collectives: 393 us -> 130 us  [the longest x1 79.6 us: on_device(): lax.all_to_all(send, 'expert', split_axis=1, concat_axis=1, tiled=True)]
    pallas_call x0 -> x2, Pallas kernels: none -> 20.7 us  [the longest x1 17.9 us: on_device(): pl.pallas_call(expert_kernel, name='expert_grad', grid=(tensor,), out_sha...]
    all_gather x1 -> x3, waiting for transfers between devices: 64.1 us -> 43.5 us  [the longest x1 41.9 us: on_device(): down_all = lax.all_gather(down_weight, 'tensor', axis=0, tiled=True)]
    dot_general x7 -> x1, matrix products: 16.5 us -> 1.03 us  [on_device(): lax.dot_general(comb, returned, (((0,), (0,)), ((), ())), preferred_eleme...]
  transfers between devices with their start and end apart: 1 -> 3, of which waited for: 1 -> 2; matrix products, arithmetic and copies ran while one was open for 0% -> 2% of each run, Pallas kernels for 0% -> 1%
where the time goes in v1:
time: 218 us; the launch traced here: 216 us
  blocking collectives  130 us (60%)
  waiting for transfers between devices  45.6 us (21%)
  Pallas kernels  20.7 us (9%)
  between operations  13.1 us (6%)
  local copies, waits for them, and re-layouts  5.38 us (2%)
    all_to_all x1, blocking collectives, on_device(): lax.all_to_all(send, 'expert', split_axis=1, concat_axis=1, tiled=True)  79.6 us
    all_to_all x1, blocking collectives, on_device(): lax.all_to_all(result.reshape(slots, 8, lanes), 'expert', split_axis=0, c...  50.5 us
    all_gather x1, waiting for transfers between devices, on_device(): down_all = lax.all_gather(down_weight, 'tensor', axis=0, tiled=True)  41.9 us
    pallas_call x1, Pallas kernels, on_device(): pl.pallas_call(expert_kernel, name='expert_grad', grid=(tensor,), out_sha...  17.9 us
  transfers between devices with their start and end apart: 3, of which 2 were waited for; matrix products, arithmetic and copies ran while one was open for 2% of the time, Pallas kernels for 1%

profile of v1, /device:TPU:1, one launch (start us, length us, event | category | flops | bytes accessed | tf_op | source)
XLA Modules:
  0.0 216.0 jit_solution(2507734826976937498)
XLA Ops:
  6.5 0.0 all-gather.4.cloned.1.call-start
  6.5 0.7 all-gather.4.cloned.1.call-update
  7.3 0.0 all-gather.6.cloned.1.call-start
  7.3 0.7 all-gather.6.cloned.1.call-update
  8.0 0.0 all-gather.8.cloned.1.call-start
  8.1 0.7 all-gather.8.cloned.1.call-update
  8.7 2.8 %route.1 = (bf16[2,320,1024]{2,1,0:T(8,128)(2,1)}, bf16[320,128]{1,0:T(8,128)(2,1)}) custom-call(bf16[128,1024]{1,0:T(8,128)(2,1)} %refs_0_.1, bf16[128,1024]{1,0:T(8,128)(2,1)} %refs_1_.1, s32[2,128]{1,0:T(2,128)} %bitcast.12, s32[2,128]{1,0:T(2,128)} %bitcast.13), custom_call_target="tpu_custom_call" | custom-call | tf_op jit(solution)/shard_map/route/pallas_call | solution.py:79
  11.6 2.7 %copy.8 = bf16[2,320,1024]{2,0,1:T(2,128)(2,1)S(1)} copy(bf16[2,320,1024]{2,1,0:T(8,128)(2,1)} %get-tuple-element.8) | data formatting | bytes 2621440 | tf_op jit(solution)/shard_map/route/pallas_call | solution.py:79
  14.2 79.6 %all_to_all.10 = bf16[2,320,1024]{2,0,1:T(2,128)(2,1)S(1)} all-to-all(bf16[2,320,1024]{2,0,1:T(2,128)(2,1)S(1)} %copy.8), channel_id=1, replica_groups=mesh['expert'=64,'tensor'=8] {'expert'}, dimensions={1} | all-to-all | bytes 2621440 | tf_op jit(solution)/shard_map/all_to_all | solution.py:89
  93.8 1.5 copy.9.rows_ref
  95.3 0.0 all-gather.4.cloned.1.call-done.gate_ref
  95.3 1.6 all-gather.6.cloned.1.call-done.up_ref
  96.8 41.9 %all-gather.8.cloned.1.call-done.down_ref = bf16[8,1024,256]{2,1,0:T(8,128)(2,1)} async-done(((bf16[1,1024,256]{2,1,0:T(8,128)(2,1)}), bf16[8,1024,256]{2,1,0:T(8,128)(2,1)}) %all-gather.8.cloned.1.call-update) | async-done | bytes 4194320 | tf_op jit(solution)/shard_map/all_gather | solution.py:77
  138.8 17.9 %expert_grad.1 = bf16[320,1024]{1,0:T(8,128)(2,1)} custom-call(bf16[2,320,1024]{2,1,0:T(8,128)(2,1)} %copy.9.rows_ref, bf16[8,1024,256]{2,1,0:T(8,128)(2,1)} %all-gather.4.cloned.1.call-done.gate_ref, bf16[8,1024,256]{2,1,0:T(8,128)(2,1)} %all-gather.6.cloned.1.call-done.up_ref, bf16[8,1024,256]{2,1,0:T(8,128)(2,1)} %all-gather.8.cloned.1.call-done.down_ref), custom_call_target="tpu_custom_call" | custom-call | tf_op jit(solution)/shard_map/expert_grad/pallas_call | solution.py:91
  156.7 0.0 copy-start
  156.7 1.2 copy.10
  157.9 50.5 %all_to_all.11 = bf16[320,8,128]{2,1,0:T(8,128)(2,1)S(1)} all-to-all(bf16[320,8,128]{2,1,0:T(8,128)(2,1)S(1)} %bitcast.11), channel_id=1, replica_groups=mesh['expert'=64,'tensor'=8] {'expert'}, dimensions={0} | all-to-all | bytes 1310720 | tf_op jit(solution)/shard_map/all_to_all | solution.py:102
  208.4 0.0 copy-done
  208.4 1.0 convolution_convert_fusion
Async XLA Ops:
  6.5 88.7 %all-gather.4.cloned.1.call-start = ((), (), s32[]{:S(2)}) async-start(), calls=%async_computation.2 | async-start | bytes 4718592 | tf_op jit(solution)/shard_map/all_gather | solution.py:75
  7.3 89.6 %all-gather.6.cloned.1.call-start = ((), (), s32[]{:S(2)}) async-start(), calls=%async_computation.3 | async-start | bytes 4718592 | tf_op jit(solution)/shard_map/all_gather | solution.py:76
  8.0 130.8 %all-gather.8.cloned.1.call-start = ((), (), s32[]{:S(2)}) async-start(), calls=%async_computation.4 | async-start | bytes 4718592 | tf_op jit(solution)/shard_map/all_gather | solution.py:77
  156.7 51.7 %copy-start = (bf16[320,128]{1,0:T(8,128)(2,1)S(1)}, bf16[320,128]{1,0:T(8,128)(2,1)}, u32[]{:S(2)}) copy-start(bf16[320,128]{1,0:T(8,128)(2,1)} %get-tuple-element.7) | copy-start | bytes 245764
Sparse Core Ops, SparseCore 0:
  9.5 45.3 all-gather.3
  57.1 39.7 all-gather.5
  99.0 39.7 all-gather.7

commit v2 on v1

--- a/solution.py
+++ b/solution.py
@@ -38,19 +38,22 @@
     send_ref[1] = jnp.dot(pick, grad_ref[...], preferred_element_type=jnp.float32).astype(jnp.bfloat16)
 
 
-def expert_kernel(rows_ref, gate_ref, up_ref, down_ref, out_ref, acc_ref):
+def expert_kernel(rows_ref, weights_ref, out_ref, acc_ref):
+    gate_cols = weights_ref[0, 0]
+    up_cols = weights_ref[0, 1]
+    down_cols = weights_ref[0, 2]
     block = pl.program_id(0)
     rows = rows_ref[0]
     grads = rows_ref[1]
-    gate_pre = jnp.dot(rows, gate_ref[0], preferred_element_type=jnp.float32)
-    up_pre = jnp.dot(rows, up_ref[0], preferred_element_type=jnp.float32)
-    hidden_grad = jnp.dot(grads, down_ref[0], preferred_element_type=jnp.float32)
+    gate_pre = jnp.dot(rows, gate_cols, preferred_element_type=jnp.float32)
+    up_pre = jnp.dot(rows, up_cols, preferred_element_type=jnp.float32)
+    hidden_grad = jnp.dot(grads, down_cols, preferred_element_type=jnp.float32)
     sig = jax.nn.sigmoid(gate_pre)
     up_grad = (hidden_grad * gate_pre * sig).astype(jnp.bfloat16)
     gate_grad = (hidden_grad * up_pre * sig * (1.0 + gate_pre * (1.0 - sig))).astype(jnp.bfloat16)
     back = (((1,), (1,)), ((), ()))
-    part = lax.dot_general(gate_grad, gate_ref[0], back, preferred_element_type=jnp.float32)
-    part = part + lax.dot_general(up_grad, up_ref[0], back, preferred_element_type=jnp.float32)
+    part = lax.dot_general(gate_grad, gate_cols, back, preferred_element_type=jnp.float32)
+    part = part + lax.dot_general(up_grad, up_cols, back, preferred_element_type=jnp.float32)
 
     @pl.when(block == 0)
     def _():
@@ -72,9 +75,8 @@
     capacity = 5
     slots = experts * capacity
     cols = gate_weight.shape[2]
-    gate_all = lax.all_gather(gate_weight, "tensor", axis=0, tiled=True)
-    up_all = lax.all_gather(up_weight, "tensor", axis=0, tiled=True)
-    down_all = lax.all_gather(down_weight, "tensor", axis=0, tiled=True)
+    weights = jnp.concatenate([gate_weight, up_weight, down_weight], axis=0)
+    weights_all = lax.all_gather(weights, "tensor", axis=0, tiled=False)
     vmem = pl.BlockSpec(memory_space=pltpu.VMEM)
     send, comb = pl.pallas_call(
         lambda *refs: route_kernel(capacity, experts, *refs),
@@ -87,17 +89,16 @@
         out_specs=(vmem, vmem),
     )(tokens, out_grad, expert_ids.T, gate_levels.T)
     received = lax.all_to_all(send, "expert", split_axis=1, concat_axis=1, tiled=True)
-    weight_spec = pl.BlockSpec((1, width, cols), lambda b: (b, 0, 0))
     result = pl.pallas_call(
         expert_kernel,
         name="expert_grad",
         grid=(tensor,),
         out_shape=jax.ShapeDtypeStruct((slots, width), jnp.bfloat16),
-        in_specs=[pl.BlockSpec((2, slots, width), lambda b: (0, 0, 0)), weight_spec, weight_spec, weight_spec],
+        in_specs=[pl.BlockSpec((2, slots, width), lambda b: (0, 0, 0)), pl.BlockSpec((1, 3, width, cols), lambda b: (b, 0, 0, 0))],
         out_specs=pl.BlockSpec((slots, width), lambda b: (0, 0)),
         scratch_shapes=[pltpu.VMEM((slots, width), jnp.float32)],
         compiler_params=pltpu.CompilerParams(vmem_limit_bytes=vmem_limit),
-    )(received, gate_all, up_all, down_all)
+    )(received, weights_all)
     lanes = width // 8
     returned = lax.all_to_all(result.reshape(slots, 8, lanes), "expert", split_axis=0, concat_axis=0, tiled=True)
     returned = returned.reshape(slots, width)

time: 218 us -> 171 us (0.78)
  waiting for transfers between devices: 45.6 us -> 0.02 us
  blocking collectives: 130 us -> 126 us
  other arithmetic: 0 us -> 2.72 us
    all_gather x3 -> x1, waiting for transfers between devices: 43.5 us -> 0.01 us  [on_device(): weights_all = lax.all_gather(weights, 'tensor', axis=0, tiled=False)]
    all_to_all x1, blocking collectives: 50.5 us -> 46 us  [on_device(): lax.all_to_all(result.reshape(slots, 8, lanes), 'expert', split_axis=0, c...]
    concatenate x0 -> x1, other arithmetic: none -> 2.72 us  [on_device(): weights = jnp.concatenate([gate_weight, up_weight, down_weight], axis=0)]
  transfers between devices with their start and end apart: 3 -> 1, of which waited for: 2 -> 0; matrix products, arithmetic and copies ran while one was open for 2% -> 2% of each run, Pallas kernels for 1% -> 2%
where the time goes in v2:
time: 171 us; the launch traced here: 169 us
  blocking collectives  126 us (74%)
  Pallas kernels  20.5 us (12%)
  between operations  13.4 us (8%)
  local copies, waits for them, and re-layouts  5.34 us (3%)
  other arithmetic  2.72 us (2%)
    all_to_all x1, blocking collectives, on_device(): lax.all_to_all(send, 'expert', split_axis=1, concat_axis=1, tiled=True)  79.6 us
    all_to_all x1, blocking collectives, on_device(): lax.all_to_all(result.reshape(slots, 8, lanes), 'expert', split_axis=0, c...  46 us
    pallas_call x1, Pallas kernels, on_device(): pl.pallas_call(expert_kernel, name='expert_grad', grid=(tensor,), out_sha...  17.7 us
  transfers between devices with their start and end apart: 1, of which 0 were waited for; matrix products, arithmetic and copies ran while one was open for 2% of the time, Pallas kernels for 2%

profile of v2, /device:TPU:1, one launch (start us, length us, event | category | flops | bytes accessed | tf_op | source)
XLA Modules:
  0.0 168.6 jit_solution(4421577283469691413)
XLA Ops:
  6.5 0.0 all-gather.3.cloned.1.call-start
  6.5 2.7 %pad_maximum_fusion = bf16[3,1024,256]{2,1,0:T(8,128)(2,1)} fusion(bf16[1,1024,256]{2,1,0:T(8,128)(2,1)} %param.13, bf16[1,1024,256]{2,1,0:T(8,128)(2,1)} %param.12, bf16[1,1024,256]{2,1,0:T(8,128)(2,1)} %param.11), kind=kLoop, calls=%fused_computation | loop fusion | flops 1572864 | bytes 3145728 | tf_op jit(solution)/shard_map/concatenate | solution.py:78
  9.3 0.0 all-gather.3.cloned.1.call-update
  9.3 2.8 %route.1 = (bf16[2,320,1024]{2,1,0:T(8,128)(2,1)}, bf16[320,128]{1,0:T(8,128)(2,1)}) custom-call(bf16[128,1024]{1,0:T(8,128)(2,1)} %refs_0_.1, bf16[128,1024]{1,0:T(8,128)(2,1)} %refs_1_.1, s32[2,128]{1,0:T(2,128)} %bitcast.14, s32[2,128]{1,0:T(2,128)} %bitcast.15), custom_call_target="tpu_custom_call" | custom-call | tf_op jit(solution)/shard_map/route/pallas_call | solution.py:81
  12.1 2.7 %copy.8 = bf16[2,320,1024]{2,0,1:T(2,128)(2,1)S(1)} copy(bf16[2,320,1024]{2,1,0:T(8,128)(2,1)} %get-tuple-element.8) | data formatting | bytes 2621440 | tf_op jit(solution)/shard_map/route/pallas_call | solution.py:81
  14.7 79.6 %all_to_all.10 = bf16[2,320,1024]{2,0,1:T(2,128)(2,1)S(1)} all-to-all(bf16[2,320,1024]{2,0,1:T(2,128)(2,1)S(1)} %copy.8), channel_id=1, replica_groups=mesh['expert'=64,'tensor'=8] {'expert'}, dimensions={1} | all-to-all | bytes 2621440 | tf_op jit(solution)/shard_map/all_to_all | solution.py:91
  94.3 1.4 copy.9.rows_ref
  95.7 0.0 all-gather.3.cloned.1.call-done
  95.7 17.7 %expert_grad.1 = bf16[320,1024]{1,0:T(8,128)(2,1)} custom-call(bf16[2,320,1024]{2,1,0:T(8,128)(2,1)} %copy.9.rows_ref, bf16[8,3,1024,256]{3,2,1,0:T(8,128)(2,1)} %bitcast.10), custom_call_target="tpu_custom_call" | custom-call | tf_op jit(solution)/shard_map/expert_grad/pallas_call | solution.py:92
  113.5 0.0 copy-start
  113.5 1.2 copy.10
  114.7 46.0 %all_to_all.11 = bf16[320,8,128]{2,1,0:T(8,128)(2,1)S(1)} all-to-all(bf16[320,8,128]{2,1,0:T(8,128)(2,1)S(1)} %bitcast.13), channel_id=1, replica_groups=mesh['expert'=64,'tensor'=8] {'expert'}, dimensions={0} | all-to-all | bytes 1310720 | tf_op jit(solution)/shard_map/all_to_all | solution.py:103
  160.7 0.0 copy-done
  160.7 1.0 convolution_convert_fusion
Async XLA Ops:
  6.5 89.2 %all-gather.3.cloned.1.call-start = ((), (), s32[]{:S(2)}) async-start(), calls=%async_computation.2 | async-start | bytes 14155776 | tf_op jit(solution)/shard_map/all_gather | solution.py:79
  113.5 47.3 %copy-start = (bf16[320,128]{1,0:T(8,128)(2,1)S(1)}, bf16[320,128]{1,0:T(8,128)(2,1)}, u32[]{:S(2)}) copy-start(bf16[320,128]{1,0:T(8,128)(2,1)} %get-tuple-element.7) | copy-start | bytes 245764
Sparse Core Ops, SparseCore 0:
  9.5 80.6 all-gather.2

commit v3 on v1

--- a/solution.py
+++ b/solution.py
@@ -38,31 +38,57 @@
     send_ref[1] = jnp.dot(pick, grad_ref[...], preferred_element_type=jnp.float32).astype(jnp.bfloat16)
 
 
-def expert_kernel(rows_ref, gate_ref, up_ref, down_ref, out_ref, acc_ref):
-    block = pl.program_id(0)
-    rows = rows_ref[0]
-    grads = rows_ref[1]
-    gate_pre = jnp.dot(rows, gate_ref[0], preferred_element_type=jnp.float32)
-    up_pre = jnp.dot(rows, up_ref[0], preferred_element_type=jnp.float32)
-    hidden_grad = jnp.dot(grads, down_ref[0], preferred_element_type=jnp.float32)
-    sig = jax.nn.sigmoid(gate_pre)
-    up_grad = (hidden_grad * gate_pre * sig).astype(jnp.bfloat16)
-    gate_grad = (hidden_grad * up_pre * sig * (1.0 + gate_pre * (1.0 - sig))).astype(jnp.bfloat16)
+def expert_kernel(rows_ref, *refs):
+    count = len(refs) - 4
+    weights = refs[:count]
+    out_ref, acc_ref, buf_ref, sems = refs[count:]
+
+    def fetch(step):
+        return pltpu.make_async_copy(weights[step], buf_ref.at[step % 2], sems.at[step % 2])
+
+    fetch(0).start()
     back = (((1,), (1,)), ((), ()))
-    part = lax.dot_general(gate_grad, gate_ref[0], back, preferred_element_type=jnp.float32)
-    part = part + lax.dot_general(up_grad, up_ref[0], back, preferred_element_type=jnp.float32)
+    for step in range(count):
+        fetch(step).wait()
+        if step + 1 < count:
+            fetch(step + 1).start()
+        gate_cols = buf_ref[step % 2, 0]
+        up_cols = buf_ref[step % 2, 1]
+        down_cols = buf_ref[step % 2, 2]
+        gate_pre = jnp.dot(rows_ref[0], gate_cols, preferred_element_type=jnp.float32)
+        up_pre = jnp.dot(rows_ref[0], up_cols, preferred_element_type=jnp.float32)
+        hidden_grad = jnp.dot(rows_ref[1], down_cols, preferred_element_type=jnp.float32)
+        sig = jax.nn.sigmoid(gate_pre)
+        up_grad = (hidden_grad * gate_pre * sig).astype(jnp.bfloat16)
+        gate_grad = (hidden_grad * up_pre * sig * (1.0 + gate_pre * (1.0 - sig))).astype(jnp.bfloat16)
+        part = lax.dot_general(gate_grad, gate_cols, back, preferred_element_type=jnp.float32)
+        part = part + lax.dot_general(up_grad, up_cols, back, preferred_element_type=jnp.float32)
+        if step == 0:
+            acc_ref[...] = part
+        elif step + 1 < count:
+            acc_ref[...] = acc_ref[...] + part
+        else:
+            out_ref[...] = (acc_ref[...] + part).astype(jnp.bfloat16)
 
-    @pl.when(block == 0)
-    def _():
-        acc_ref[...] = part
 
-    @pl.when(block > 0)
-    def _():
-        acc_ref[...] = acc_ref[...] + part
+def gather_weights(weights):
+    core = lax.axis_index("tensor") % 2
+    chips = lax.axis_size("tensor") // 2
 
-    @pl.when(block == pl.num_programs(0) - 1)
-    def _():
-        out_ref[...] = acc_ref[...].astype(jnp.bfloat16)
+    def shift(value, step0, step1):
+        pairs = []
+        for chip in range(chips):
+            pairs.append((2 * chip, 2 * ((chip + step0) % chips)))
+            pairs.append((2 * chip + 1, 2 * ((chip + step1) % chips) + 1))
+        return lax.ppermute(value, "tensor", pairs)
+
+    def swap(value):
+        return lax.ppermute(value, "tensor", [(i, i ^ 1) for i in range(2 * chips)])
+
+    left = shift(weights, 1, 1)
+    right = shift(weights, -1, -1)
+    far = shift(jnp.where(core == 0, left, right), 1, -1)
+    return [weights, swap(weights), left, right, swap(left), swap(right), far, swap(far)]
 
 
 def on_device(tokens, out_grad, expert_ids, gate_levels, gate_weight, up_weight, down_weight):
@@ -72,9 +98,6 @@
     capacity = 5
     slots = experts * capacity
     cols = gate_weight.shape[2]
-    gate_all = lax.all_gather(gate_weight, "tensor", axis=0, tiled=True)
-    up_all = lax.all_gather(up_weight, "tensor", axis=0, tiled=True)
-    down_all = lax.all_gather(down_weight, "tensor", axis=0, tiled=True)
     vmem = pl.BlockSpec(memory_space=pltpu.VMEM)
     send, comb = pl.pallas_call(
         lambda *refs: route_kernel(capacity, experts, *refs),
@@ -87,17 +110,21 @@
         out_specs=(vmem, vmem),
     )(tokens, out_grad, expert_ids.T, gate_levels.T)
     received = lax.all_to_all(send, "expert", split_axis=1, concat_axis=1, tiled=True)
-    weight_spec = pl.BlockSpec((1, width, cols), lambda b: (b, 0, 0))
+    weights = jnp.concatenate([gate_weight, up_weight, down_weight], axis=0)
+    blocks = gather_weights(weights)
     result = pl.pallas_call(
         expert_kernel,
         name="expert_grad",
-        grid=(tensor,),
         out_shape=jax.ShapeDtypeStruct((slots, width), jnp.bfloat16),
-        in_specs=[pl.BlockSpec((2, slots, width), lambda b: (0, 0, 0)), weight_spec, weight_spec, weight_spec],
-        out_specs=pl.BlockSpec((slots, width), lambda b: (0, 0)),
-        scratch_shapes=[pltpu.VMEM((slots, width), jnp.float32)],
+        in_specs=[vmem] + [pl.BlockSpec(memory_space=pl.ANY)] * tensor,
+        out_specs=vmem,
+        scratch_shapes=[
+            pltpu.VMEM((slots, width), jnp.float32),
+            pltpu.VMEM((2,) + weights.shape, jnp.bfloat16),
+            pltpu.SemaphoreType.DMA((2,)),
+        ],
         compiler_params=pltpu.CompilerParams(vmem_limit_bytes=vmem_limit),
-    )(received, gate_all, up_all, down_all)
+    )(received, *blocks)
     lanes = width // 8
     returned = lax.all_to_all(result.reshape(slots, 8, lanes), "expert", split_axis=0, concat_axis=0, tiled=True)
     returned = returned.reshape(slots, width)

time: 218 us -> 173 us (0.79)
  blocking collectives: 130 us -> 49.4 us
  starting transfers between devices: 0.08 us -> 42.2 us
  between operations: 13.1 us -> 0.16 us
  local copies, waits for them, and re-layouts: 5.38 us -> 10.2 us
  waiting for transfers between devices: 45.6 us -> 48 us
    all_to_all x1 -> x0, blocking collectives: 79.6 us -> none  [on_device(): lax.all_to_all(send, 'expert', split_axis=1, concat_axis=1, tiled=True)]
    ppermute x0 -> x7, waiting for transfers between devices: none -> 48 us  [the longest x3 47.6 us: shift(): return lax.ppermute(value, 'tensor', pairs)]
    all_gather x3 -> x0, waiting for transfers between devices: 43.5 us -> none  [the longest x1 41.9 us: on_device(): down_all = lax.all_gather(down_weight, 'tensor', axis=0, tiled=True)]
    ppermute x0 -> x7, starting transfers between devices: none -> 22.6 us  [the longest x4 14.4 us: swap(): return lax.ppermute(value, 'tensor', [(i, i ^ 1) for i in range(2 * chips)])]
    all_to_all x0 -> x1, starting transfers between devices: none -> 19.6 us  [on_device(): lax.all_to_all(send, 'expert', split_axis=1, concat_axis=1, tiled=True)]
  transfers between devices with their start and end apart: 3 -> 8, of which waited for: 2 -> 4; matrix products, arithmetic and copies ran while one was open for 2% -> 3% of each run, Pallas kernels for 1% -> 0%
where the time goes in v3:
time: 173 us; the launch traced here: 170 us
  blocking collectives  49.4 us (29%)
  waiting for transfers between devices  48 us (28%)
  starting transfers between devices  42.2 us (24%)
  Pallas kernels  19.3 us (11%)
  local copies, waits for them, and re-layouts  10.2 us (6%)
    all_to_all x1, blocking collectives, on_device(): lax.all_to_all(result.reshape(slots, 8, lanes), 'expert', split_axis=0, c...  49.4 us
    ppermute x3, waiting for transfers between devices, shift(): return lax.ppermute(value, 'tensor', pairs)  47.6 us
    all_to_all x1, starting transfers between devices, on_device(): lax.all_to_all(send, 'expert', split_axis=1, concat_axis=1, tiled=True)  19.6 us
    pallas_call x1, Pallas kernels, on_device(): pl.pallas_call(expert_kernel, name='expert_grad', out_shape=jax.ShapeDtyp...  16.5 us
    ppermute x4, starting transfers between devices, swap(): return lax.ppermute(value, 'tensor', [(i, i ^ 1) for i in range(2 * chips)])  14.4 us
    ppermute x3, starting transfers between devices, shift(): return lax.ppermute(value, 'tensor', pairs)  8.22 us
    pallas_call x1, local copies, waits for them, and re-layouts, on_device(): pl.pallas_call(lambda *refs: route_kernel(capacity, experts, *refs), name...  3.73 us
  transfers between devices with their start and end apart: 8, of which 4 were waited for; matrix products, arithmetic and copies ran while one was open for 3% of the time, Pallas kernels for 0%

profile of v3, /device:TPU:1, one launch (start us, length us, event | category | flops | bytes accessed | tf_op | source)
XLA Modules:
  0.0 170.5 jit_solution(334723055243019925)
XLA Ops:
  0.0 2.8 %route.1 = (bf16[2,320,1024]{2,1,0:T(8,128)(2,1)}, bf16[320,128]{1,0:T(8,128)(2,1)}) custom-call(bf16[128,1024]{1,0:T(8,128)(2,1)} %refs_0_.1, bf16[128,1024]{1,0:T(8,128)(2,1)} %refs_1_.1, s32[2,128]{1,0:T(2,128)} %bitcast.12, s32[2,128]{1,0:T(2,128)} %bitcast.13), custom_call_target="tpu_custom_call" | custom-call | tf_op jit(solution)/shard_map/route/pallas_call | solution.py:102
  2.8 3.7 %copy.8 = bf16[2,320,1024]{2,0,1:T(2,128)(2,1)} copy(bf16[2,320,1024]{2,1,0:T(8,128)(2,1)} %get-tuple-element.8) | data formatting | bytes 2621440 | tf_op jit(solution)/shard_map/route/pallas_call | solution.py:102
  6.5 0.0 copy-start.2
  6.5 0.0 copy-start.3
  6.5 19.6 %all-to-all-start = ((bf16[2,320,1024]{2,0,1:T(2,128)(2,1)}), bf16[2,320,1024]{2,0,1:T(2,128)(2,1)}, u32[]{:S(2)}, u32[]{:S(2)}) async-start(bf16[2,320,1024]{2,0,1:T(2,128)(2,1)} %copy.8), calls=%async_computation | async-start | bytes 2621440 | tf_op jit(solution)/shard_map/all_to_all | solution.py:112
  26.1 0.0 copy-done.2
  26.1 0.0 copy-start.4
  26.2 0.8 constant_dynamic-update-slice_fusion.2
  27.0 0.0 copy-done.3
  27.0 0.8 constant_dynamic-update-slice_fusion.1
  27.8 0.0 copy-done.4
  27.8 0.8 constant_dynamic-update-slice_fusion.refs_0_
  28.7 4.4 %collective-permute-start.2 = (bf16[3,1024,256]{2,1,0:T(8,128)(2,1)}, bf16[3,1024,256]{2,1,0:T(8,128)(2,1)S(1)}, u32[]{:S(2)}, u32[]{:S(2)}) collective-permute-start(bf16[3,1024,256]{2,1,0:T(8,128)(2,1)} %constant_dynamic-update-slice_fusion.refs_0_), channel_id=1, source_target_pairs={{0,6},{1,7},{2,0},{3,1},{4,2},{5,3},{6,4},{7,5},{8,14},{9,15},{10,... | collective-permute-start | bytes 4718600 | tf_op jit(solution)/shard_map/ppermute | solution.py:83
  33.0 1.9 %collective-permute-start.1 = (bf16[3,1024,256]{2,1,0:T(8,128)(2,1)}, bf16[3,1024,256]{2,1,0:T(8,128)(2,1)S(1)}, u32[]{:S(2)}, u32[]{:S(2)}) collective-permute-start(bf16[3,1024,256]{2,1,0:T(8,128)(2,1)} %constant_dynamic-update-slice_fusion.refs_0_), channel_id=1, source_target_pairs={{0,2},{1,3},{2,4},{3,5},{4,6},{5,7},{6,0},{7,1},{8,10},{9,11},{10,... | collective-permute-start | bytes 4718600 | tf_op jit(solution)/shard_map/ppermute | solution.py:83
  35.0 31.2 %collective-permute-done.2.refs_3_ = bf16[3,1024,256]{2,1,0:T(8,128)(2,1)S(1)} collective-permute-done((bf16[3,1024,256]{2,1,0:T(8,128)(2,1)}, bf16[3,1024,256]{2,1,0:T(8,128)(2,1)S(1)}, u32[]{:S(2)}, u32[]{:S(2)}) %collective-permute-start.2) | collective-permute-done | bytes 1572896 | tf_op jit(solution)/shard_map/ppermute | solution.py:83
  66.1 0.0 copy-start
  66.1 5.0 %collective-permute-done.1.refs_2_ = bf16[3,1024,256]{2,1,0:T(8,128)(2,1)S(1)} collective-permute-done((bf16[3,1024,256]{2,1,0:T(8,128)(2,1)}, bf16[3,1024,256]{2,1,0:T(8,128)(2,1)S(1)}, u32[]{:S(2)}, u32[]{:S(2)}) %collective-permute-start.1) | collective-permute-done | bytes 1572896 | tf_op jit(solution)/shard_map/ppermute | solution.py:83
  71.2 0.0 copy-start.1
  71.2 0.2 broadcast_select_fusion
  71.4 1.9 %collective-permute-start.5 = (bf16[3,1024,256]{2,1,0:T(8,128)(2,1)S(1)}, bf16[3,1024,256]{2,1,0:T(8,128)(2,1)}, u32[]{:S(2)}, u32[]{:S(2)}) collective-permute-start(bf16[3,1024,256]{2,1,0:T(8,128)(2,1)S(1)} %broadcast_select_fusion), channel_id=1, source_target_pairs={{0,2},{1,7},{2,4},{3,1},{4,6},{5,3},{6,0},{7,5},{8,10},{9,15},{10,... | collective-permute-start | bytes 4718600 | tf_op jit(solution)/shard_map/ppermute | solution.py:83
  73.3 3.9 %collective-permute-start = (bf16[3,1024,256]{2,1,0:T(8,128)(2,1)}, bf16[3,1024,256]{2,1,0:T(8,128)(2,1)}, u32[]{:S(2)}, u32[]{:S(2)}) collective-permute-start(bf16[3,1024,256]{2,1,0:T(8,128)(2,1)} %constant_dynamic-update-slice_fusion.refs_0_), channel_id=1, source_target_pairs={{0,1},{1,0},{2,3},{3,2},{4,5},{5,4},{6,7},{7,6},{8,9},{9,8},{10,11... | collective-permute-start | bytes 4718600 | tf_op jit(solution)/shard_map/ppermute | solution.py:86
  77.2 0.0 copy-done
  77.2 1.9 %collective-permute-start.4 = (bf16[3,1024,256]{2,1,0:T(8,128)(2,1)S(1)}, bf16[3,1024,256]{2,1,0:T(8,128)(2,1)}, u32[]{:S(2)}, u32[]{:S(2)}) collective-permute-start(bf16[3,1024,256]{2,1,0:T(8,128)(2,1)S(1)} %collective-permute-done.2.refs_3_), channel_id=1, source_target_pairs={{0,1},{1,0},{2,3},{3,2},{4,5},{5,4},{6,7},{7,6},{8,9},{9,8},{10,11... | collective-permute-start | bytes 4718600 | tf_op jit(solution)/shard_map/ppermute | solution.py:86
  79.1 0.0 copy-done.1
  79.1 2.4 %collective-permute-start.3 = (bf16[3,1024,256]{2,1,0:T(8,128)(2,1)S(1)}, bf16[3,1024,256]{2,1,0:T(8,128)(2,1)}, u32[]{:S(2)}, u32[]{:S(2)}) collective-permute-start(bf16[3,1024,256]{2,1,0:T(8,128)(2,1)S(1)} %collective-permute-done.1.refs_2_), channel_id=1, source_target_pairs={{0,1},{1,0},{2,3},{3,2},{4,5},{5,4},{6,7},{7,6},{8,9},{9,8},{10,11... | collective-permute-start | bytes 4718600 | tf_op jit(solution)/shard_map/ppermute | solution.py:86
  81.6 11.4 %collective-permute-done.5.refs_6_ = bf16[3,1024,256]{2,1,0:T(8,128)(2,1)} collective-permute-done((bf16[3,1024,256]{2,1,0:T(8,128)(2,1)S(1)}, bf16[3,1024,256]{2,1,0:T(8,128)(2,1)}, u32[]{:S(2)}, u32[]{:S(2)}) %collective-permute-start.5) | collective-permute-done | bytes 1572896 | tf_op jit(solution)/shard_map/ppermute | solution.py:83
  92.9 6.1 %collective-permute-start.6 = (bf16[3,1024,256]{2,1,0:T(8,128)(2,1)}, bf16[3,1024,256]{2,1,0:T(8,128)(2,1)}, u32[]{:S(2)}, u32[]{:S(2)}) collective-permute-start(bf16[3,1024,256]{2,1,0:T(8,128)(2,1)} %collective-permute-done.5.refs_6_), channel_id=1, source_target_pairs={{0,1},{1,0},{2,3},{3,2},{4,5},{5,4},{6,7},{7,6},{8,9},{9,8},{10,11... | collective-permute-start | bytes 4718600 | tf_op jit(solution)/shard_map/ppermute | solution.py:86
  99.1 0.0 all-to-all-done
  99.1 2.7 %copy.9.rows_ref = bf16[2,320,1024]{2,1,0:T(8,128)(2,1)} copy(bf16[2,320,1024]{2,0,1:T(2,128)(2,1)} %all-to-all-done) | data formatting | bytes 2621440 | tf_op jit(solution)/shard_map/all_to_all | solution.py:112
  101.8 0.0 collective-permute-done.refs_1_
  101.8 0.0 collective-permute-done.4.refs_5_
  101.8 0.0 collective-permute-done.3.refs_4_
  101.8 0.4 collective-permute-done.6.refs_7_
  102.2 16.5 %expert_grad.1 = bf16[320,1024]{1,0:T(8,128)(2,1)} custom-call(bf16[2,320,1024]{2,1,0:T(8,128)(2,1)} %copy.9.rows_ref, bf16[3,1024,256]{2,1,0:T(8,128)(2,1)} %constant_dynamic-update-slice_fusion.refs_0_, bf16[3,1024,256]{2,1,0:T(8,128)(2,1)} %collective-permute-done.refs_1_, bf16[3,1024,256]{2,1,0:T(8,128)(2,1)} %copy-done.1, ...), custom_call_target="tpu_custom_call" | custom-call | tf_op jit(solution)/shard_map/expert_grad/pallas_call | solution.py:115
  118.8 0.0 copy-start.5
  118.8 1.2 copy.10
  120.0 49.4 %all_to_all.10 = bf16[320,8,128]{2,1,0:T(8,128)(2,1)S(1)} all-to-all(bf16[320,8,128]{2,1,0:T(8,128)(2,1)S(1)} %bitcast.11), channel_id=1, replica_groups=mesh['expert'=64,'tensor'=8] {'expert'}, dimensions={0} | all-to-all | bytes 1310720 | tf_op jit(solution)/shard_map/all_to_all | solution.py:129
  169.4 0.0 copy-done.5
  169.4 1.0 convolution_convert_fusion
Async XLA Ops:
  6.5 19.7 %copy-start.2 = (bf16[1,1024,256]{2,1,0:T(8,128)(2,1)S(1)}, bf16[1,1024,256]{2,1,0:T(8,128)(2,1)}, u32[]{:S(2)}) copy-start(bf16[1,1024,256]{2,1,0:T(8,128)(2,1)} %param.11) | copy-start | bytes 1572868
  6.5 20.5 %copy-start.3 = (bf16[1,1024,256]{2,1,0:T(8,128)(2,1)S(1)}, bf16[1,1024,256]{2,1,0:T(8,128)(2,1)}, u32[]{:S(2)}) copy-start(bf16[1,1024,256]{2,1,0:T(8,128)(2,1)} %param.12) | copy-start | bytes 1572868
  6.5 92.6 %all-to-all-start = ((bf16[2,320,1024]{2,0,1:T(2,128)(2,1)}), bf16[2,320,1024]{2,0,1:T(2,128)(2,1)}, u32[]{:S(2)}, u32[]{:S(2)}) async-start(bf16[2,320,1024]{2,0,1:T(2,128)(2,1)} %copy.8), calls=%async_computation | async-start | bytes 2621440 | tf_op jit(solution)/shard_map/all_to_all | solution.py:112
  26.1 1.7 copy-start.4
  28.7 37.5 %collective-permute-start.2 = (bf16[3,1024,256]{2,1,0:T(8,128)(2,1)}, bf16[3,1024,256]{2,1,0:T(8,128)(2,1)S(1)}, u32[]{:S(2)}, u32[]{:S(2)}) collective-permute-start(bf16[3,1024,256]{2,1,0:T(8,128)(2,1)} %constant_dynamic-update-slice_fusion.refs_0_), channel_id=1, source_target_pairs={{0,6},{1,7},{2,0},{3,1},{4,2},{5,3},{6,4},{7,5},{8,14},{9,15},{10,... | collective-permute-start | bytes 4718600 | tf_op jit(solution)/shard_map/ppermute | solution.py:83
  33.0 38.1 %collective-permute-start.1 = (bf16[3,1024,256]{2,1,0:T(8,128)(2,1)}, bf16[3,1024,256]{2,1,0:T(8,128)(2,1)S(1)}, u32[]{:S(2)}, u32[]{:S(2)}) collective-permute-start(bf16[3,1024,256]{2,1,0:T(8,128)(2,1)} %constant_dynamic-update-slice_fusion.refs_0_), channel_id=1, source_target_pairs={{0,2},{1,3},{2,4},{3,5},{4,6},{5,7},{6,0},{7,1},{8,10},{9,11},{10,... | collective-permute-start | bytes 4718600 | tf_op jit(solution)/shard_map/ppermute | solution.py:83
  66.1 11.0 %copy-start = (bf16[3,1024,256]{2,1,0:T(8,128)(2,1)}, bf16[3,1024,256]{2,1,0:T(8,128)(2,1)S(1)}, u32[]{:S(2)}) copy-start(bf16[3,1024,256]{2,1,0:T(8,128)(2,1)S(1)} %collective-permute-done.2.refs_3_) | copy-start | bytes 4718596
  71.2 7.9 %copy-start.1 = (bf16[3,1024,256]{2,1,0:T(8,128)(2,1)}, bf16[3,1024,256]{2,1,0:T(8,128)(2,1)S(1)}, u32[]{:S(2)}) copy-start(bf16[3,1024,256]{2,1,0:T(8,128)(2,1)S(1)} %collective-permute-done.1.refs_2_) | copy-start | bytes 4718596
  71.4 21.6 %collective-permute-start.5 = (bf16[3,1024,256]{2,1,0:T(8,128)(2,1)S(1)}, bf16[3,1024,256]{2,1,0:T(8,128)(2,1)}, u32[]{:S(2)}, u32[]{:S(2)}) collective-permute-start(bf16[3,1024,256]{2,1,0:T(8,128)(2,1)S(1)} %broadcast_select_fusion), channel_id=1, source_target_pairs={{0,2},{1,7},{2,4},{3,1},{4,6},{5,3},{6,0},{7,5},{8,10},{9,15},{10,... | collective-permute-start | bytes 4718600 | tf_op jit(solution)/shard_map/ppermute | solution.py:83
  73.3 28.5 %collective-permute-start = (bf16[3,1024,256]{2,1,0:T(8,128)(2,1)}, bf16[3,1024,256]{2,1,0:T(8,128)(2,1)}, u32[]{:S(2)}, u32[]{:S(2)}) collective-permute-start(bf16[3,1024,256]{2,1,0:T(8,128)(2,1)} %constant_dynamic-update-slice_fusion.refs_0_), channel_id=1, source_target_pairs={{0,1},{1,0},{2,3},{3,2},{4,5},{5,4},{6,7},{7,6},{8,9},{9,8},{10,11... | collective-permute-start | bytes 4718600 | tf_op jit(solution)/shard_map/ppermute | solution.py:86
  77.2 24.6 %collective-permute-start.4 = (bf16[3,1024,256]{2,1,0:T(8,128)(2,1)S(1)}, bf16[3,1024,256]{2,1,0:T(8,128)(2,1)}, u32[]{:S(2)}, u32[]{:S(2)}) collective-permute-start(bf16[3,1024,256]{2,1,0:T(8,128)(2,1)S(1)} %collective-permute-done.2.refs_3_), channel_id=1, source_target_pairs={{0,1},{1,0},{2,3},{3,2},{4,5},{5,4},{6,7},{7,6},{8,9},{9,8},{10,11... | collective-permute-start | bytes 4718600 | tf_op jit(solution)/shard_map/ppermute | solution.py:86
  79.1 22.7 %collective-permute-start.3 = (bf16[3,1024,256]{2,1,0:T(8,128)(2,1)S(1)}, bf16[3,1024,256]{2,1,0:T(8,128)(2,1)}, u32[]{:S(2)}, u32[]{:S(2)}) collective-permute-start(bf16[3,1024,256]{2,1,0:T(8,128)(2,1)S(1)} %collective-permute-done.1.refs_2_), channel_id=1, source_target_pairs={{0,1},{1,0},{2,3},{3,2},{4,5},{5,4},{6,7},{7,6},{8,9},{9,8},{10,11... | collective-permute-start | bytes 4718600 | tf_op jit(solution)/shard_map/ppermute | solution.py:86
  92.9 9.3 %collective-permute-start.6 = (bf16[3,1024,256]{2,1,0:T(8,128)(2,1)}, bf16[3,1024,256]{2,1,0:T(8,128)(2,1)}, u32[]{:S(2)}, u32[]{:S(2)}) collective-permute-start(bf16[3,1024,256]{2,1,0:T(8,128)(2,1)} %collective-permute-done.5.refs_6_), channel_id=1, source_target_pairs={{0,1},{1,0},{2,3},{3,2},{4,5},{5,4},{6,7},{7,6},{8,9},{9,8},{10,11... | collective-permute-start | bytes 4718600 | tf_op jit(solution)/shard_map/ppermute | solution.py:86
  118.8 50.7 %copy-start.5 = (bf16[320,128]{1,0:T(8,128)(2,1)S(1)}, bf16[320,128]{1,0:T(8,128)(2,1)}, u32[]{:S(2)}) copy-start(bf16[320,128]{1,0:T(8,128)(2,1)} %get-tuple-element.7) | copy-start | bytes 245764

commit v4 on v3

--- a/solution.py
+++ b/solution.py
@@ -5,11 +5,20 @@
 from jax.experimental.pallas import tpu as pltpu
 from jax.sharding import PartitionSpec as P
 
+
 level_scale = 1.0 / 256.0
 vmem_limit = 56 * 1024 * 1024
+groups = 8
 
 
-def route_kernel(capacity, experts, tok_ref, grad_ref, ids_ref, lev_ref, send_ref, comb_ref):
+def route_kernel(capacity, experts, *refs):
+    tok_ref, grad_ref, ids_ref, lev_ref, gate_ref, up_ref, down_ref = refs[:7]
+    send_ref, comb_ref, stack_ref, stage_ref, buf_ref, sems = refs[7:]
+    weights = (gate_ref, up_ref, down_ref)
+    loads = [pltpu.make_async_copy(ref.at[0], buf_ref.at[i], sems.at[0, i]) for i, ref in enumerate(weights)]
+    stores = [pltpu.make_async_copy(buf_ref.at[i], stack_ref.at[i], sems.at[1, i]) for i in range(3)]
+    for load in loads:
+        load.start()
     count = ids_ref.shape[1]
     slots = comb_ref.shape[0]
     ids0 = ids_ref[0:1, :]
@@ -34,19 +43,33 @@
     comb = jnp.where(at0, scale[0:1, :], 0.0) + jnp.where(at1, scale[1:2, :], 0.0)
     comb_ref[...] = comb.astype(jnp.bfloat16)
     pick = jnp.where(at0 | at1, 1.0, 0.0).astype(jnp.bfloat16)
-    send_ref[0] = jnp.dot(pick, tok_ref[...], preferred_element_type=jnp.float32).astype(jnp.bfloat16)
-    send_ref[1] = jnp.dot(pick, grad_ref[...], preferred_element_type=jnp.float32).astype(jnp.bfloat16)
+    for load, store in zip(loads, stores):
+        load.wait()
+        store.start()
+    for half, source in enumerate((tok_ref, grad_ref)):
+        rows = jnp.dot(pick, source[...], preferred_element_type=jnp.float32)
+        for c in range(groups):
+            stage_ref[pl.ds(half * groups + c, slots, stride=2 * groups), :] = rows[:, c * 128:(c + 1) * 128]
+    send_ref[...] = stage_ref[...].astype(jnp.bfloat16)
+    for store in stores:
+        store.wait()
 
 
 def expert_kernel(rows_ref, *refs):
-    count = len(refs) - 4
+    count = len(refs) - 7
     weights = refs[:count]
-    out_ref, acc_ref, buf_ref, sems = refs[count:]
+    out_ref, acc_ref, buf_ref, stage_ref, tok_ref, grad_ref, sems = refs[count:]
+    slots = acc_ref.shape[0]
 
     def fetch(step):
         return pltpu.make_async_copy(weights[step], buf_ref.at[step % 2], sems.at[step % 2])
 
     fetch(0).start()
+    stage_ref[...] = rows_ref[...].astype(jnp.float32)
+    for half, target in enumerate((tok_ref, grad_ref)):
+        for c in range(groups):
+            part = stage_ref[pl.ds(half * groups + c, slots, stride=2 * groups), :]
+            target[:, c * 128:(c + 1) * 128] = part.astype(jnp.bfloat16)
     back = (((1,), (1,)), ((), ()))
     for step in range(count):
         fetch(step).wait()
@@ -55,9 +78,9 @@
         gate_cols = buf_ref[step % 2, 0]
         up_cols = buf_ref[step % 2, 1]
         down_cols = buf_ref[step % 2, 2]
-        gate_pre = jnp.dot(rows_ref[0], gate_cols, preferred_element_type=jnp.float32)
-        up_pre = jnp.dot(rows_ref[0], up_cols, preferred_element_type=jnp.float32)
-        hidden_grad = jnp.dot(rows_ref[1], down_cols, preferred_element_type=jnp.float32)
+        gate_pre = jnp.dot(tok_ref[...], gate_cols, preferred_element_type=jnp.float32)
+        up_pre = jnp.dot(tok_ref[...], up_cols, preferred_element_type=jnp.float32)
+        hidden_grad = jnp.dot(grad_ref[...], down_cols, preferred_element_type=jnp.float32)
         sig = jax.nn.sigmoid(gate_pre)
         up_grad = (hidden_grad * gate_pre * sig).astype(jnp.bfloat16)
         gate_grad = (hidden_grad * up_pre * sig * (1.0 + gate_pre * (1.0 - sig))).astype(jnp.bfloat16)
@@ -65,10 +88,12 @@
         part = part + lax.dot_general(up_grad, up_cols, back, preferred_element_type=jnp.float32)
         if step == 0:
             acc_ref[...] = part
-        elif step + 1 < count:
+        else:
             acc_ref[...] = acc_ref[...] + part
-        else:
-            out_ref[...] = (acc_ref[...] + part).astype(jnp.bfloat16)
+    out_rows = slots * groups
+    for c in range(groups):
+        stage_ref[pl.ds(c, slots, stride=groups), :] = acc_ref[:, c * 128:(c + 1) * 128]
+    out_ref[...] = stage_ref[0:out_rows, :].astype(jnp.bfloat16)
 
 
 def gather_weights(weights):
@@ -97,36 +122,47 @@
     tensor = lax.axis_size("tensor")
     capacity = 5
     slots = experts * capacity
-    cols = gate_weight.shape[2]
     vmem = pl.BlockSpec(memory_space=pltpu.VMEM)
-    send, comb = pl.pallas_call(
+    hbm = pl.BlockSpec(memory_space=pl.ANY)
+    lanes = width // groups
+    stack_shape = (3,) + gate_weight.shape[1:]
+    send, comb, weights = pl.pallas_call(
         lambda *refs: route_kernel(capacity, experts, *refs),
         name="route",
         out_shape=(
-            jax.ShapeDtypeStruct((2, slots, width), jnp.bfloat16),
+            jax.ShapeDtypeStruct((slots * 2 * groups, lanes), jnp.bfloat16),
             jax.ShapeDtypeStruct((slots, tok_count), jnp.bfloat16),
+            jax.ShapeDtypeStruct(stack_shape, jnp.bfloat16),
         ),
-        in_specs=[vmem] * 4,
-        out_specs=(vmem, vmem),
-    )(tokens, out_grad, expert_ids.T, gate_levels.T)
-    received = lax.all_to_all(send, "expert", split_axis=1, concat_axis=1, tiled=True)
-    weights = jnp.concatenate([gate_weight, up_weight, down_weight], axis=0)
+        in_specs=[vmem] * 4 + [hbm] * 3,
+        out_specs=(vmem, vmem, hbm),
+        scratch_shapes=[
+            pltpu.VMEM((slots * 2 * groups, lanes), jnp.float32),
+            pltpu.VMEM(stack_shape, jnp.bfloat16),
+            pltpu.SemaphoreType.DMA((2, 3)),
+        ],
+        compiler_params=pltpu.CompilerParams(vmem_limit_bytes=vmem_limit),
+    )(tokens, out_grad, expert_ids.T, gate_levels.T, gate_weight, up_weight, down_weight)
+    received = lax.all_to_all(send, "expert", split_axis=0, concat_axis=0, tiled=True)
     blocks = gather_weights(weights)
     result = pl.pallas_call(
         expert_kernel,
         name="expert_grad",
-        out_shape=jax.ShapeDtypeStruct((slots, width), jnp.bfloat16),
-        in_specs=[vmem] + [pl.BlockSpec(memory_space=pl.ANY)] * tensor,
+        out_shape=jax.ShapeDtypeStruct((slots * groups, lanes), jnp.bfloat16),
+        in_specs=[vmem] + [hbm] * tensor,
         out_specs=vmem,
         scratch_shapes=[
             pltpu.VMEM((slots, width), jnp.float32),
-            pltpu.VMEM((2,) + weights.shape, jnp.bfloat16),
+            pltpu.VMEM((2,) + stack_shape, jnp.bfloat16),
+            pltpu.VMEM((slots * 2 * groups, lanes), jnp.float32),
+            pltpu.VMEM((slots, width), jnp.bfloat16),
+            pltpu.VMEM((slots, width), jnp.bfloat16),
             pltpu.SemaphoreType.DMA((2,)),
         ],
         compiler_params=pltpu.CompilerParams(vmem_limit_bytes=vmem_limit),
     )(received, *blocks)
-    lanes = width // 8
-    returned = lax.all_to_all(result.reshape(slots, 8, lanes), "expert", split_axis=0, concat_axis=0, tiled=True)
+    result = result.reshape(slots, groups, lanes)
+    returned = lax.all_to_all(result, "expert", split_axis=0, concat_axis=0, tiled=True)
     returned = returned.reshape(slots, width)
     total = lax.dot_general(comb, returned, (((0,), (0,)), ((), ())), preferred_element_type=jnp.float32)
     return total.astype(jnp.bfloat16)

time: 173 us -> 167 us (0.965)
  local copies, waits for them, and re-layouts: 10.2 us -> 2.86 us
  Pallas kernels: 19.3 us -> 21.1 us
    pallas_call x1 -> x0, local copies, waits for them, and re-layouts: 3.73 us -> none  [on_device(): pl.pallas_call(lambda *refs: route_kernel(capacity, experts, *refs), name...]
    all_to_all x1 -> x0, local copies, waits for them, and re-layouts: 2.74 us -> none  [on_device(): lax.all_to_all(send, 'expert', split_axis=1, concat_axis=1, tiled=True)]
    pallas_call x1, Pallas kernels: 2.76 us -> 4.52 us  [on_device(): pl.pallas_call(lambda *refs: route_kernel(capacity, experts, *refs), name...]
  transfers between devices with their start and end apart: 8 -> 8, of which waited for: 4 -> 4; matrix products, arithmetic and copies ran while one was open for 3% -> 0% of each run, Pallas kernels for 0% -> 0%
where the time goes in v4:
time: 167 us; the launch traced here: 165 us
  blocking collectives  49.6 us (30%)
  waiting for transfers between devices  47.6 us (29%)
  starting transfers between devices  42 us (25%)
  Pallas kernels  21.1 us (13%)
  local copies, waits for them, and re-layouts  2.86 us (2%)
    all_to_all x1, blocking collectives, on_device(): lax.all_to_all(result, 'expert', split_axis=0, concat_axis=0, tiled=True)  49.6 us
    ppermute x3, waiting for transfers between devices, shift(): return lax.ppermute(value, 'tensor', pairs)  47.6 us
    all_to_all x1, starting transfers between devices, on_device(): lax.all_to_all(send, 'expert', split_axis=0, concat_axis=0, tiled=True)  19.5 us
    pallas_call x1, Pallas kernels, on_device(): pl.pallas_call(expert_kernel, name='expert_grad', out_shape=jax.ShapeDtyp...  16.6 us
    ppermute x4, starting transfers between devices, swap(): return lax.ppermute(value, 'tensor', [(i, i ^ 1) for i in range(2 * chips)])  14.2 us
    ppermute x3, starting transfers between devices, shift(): return lax.ppermute(value, 'tensor', pairs)  8.23 us
    pallas_call x1, Pallas kernels, on_device(): pl.pallas_call(lambda *refs: route_kernel(capacity, experts, *refs), name...  4.52 us
  transfers between devices with their start and end apart: 8, of which 4 were waited for; matrix products, arithmetic and copies ran while one was open for 0% of the time, Pallas kernels for 0%

profile of v4, /device:TPU:1, one launch (start us, length us, event | category | flops | bytes accessed | tf_op | source)
XLA Modules:
  0.0 164.6 jit_solution(18229265342253268837)
XLA Ops:
  0.0 4.5 %route.1 = (bf16[5120,128]{1,0:T(8,128)(2,1)}, bf16[320,128]{1,0:T(8,128)(2,1)}, bf16[3,1024,256]{2,1,0:T(8,128)(2,1)}) custom-call(bf16[128,1024]{1,0:T(8,128)(2,1)} %refs_0_.1, bf16[128,1024]{1,0:T(8,128)(2,1)} %refs_1_.1, s32[2,128]{1,0:T(2,128)} %bitcast.13, s32[2,128]{1,0:T(2,128)} %bitcast.14, bf16[1,1024,256]{2,1,0:T(8,128)(2,1)} %refs_4_.1, ...), custom_call_target="tpu_custom_call" | custom-call | tf_op jit(solution)/shard_map/route/pallas_call | solution.py:129
  4.5 19.5 %all-to-all-start = ((bf16[64,80,128]{2,1,0:T(8,128)(2,1)}), bf16[64,80,128]{2,1,0:T(8,128)(2,1)}, u32[]{:S(2)}, u32[]{:S(2)}) async-start(bf16[64,80,128]{2,1,0:T(8,128)(2,1)} %bitcast.12), calls=%async_computation | async-start | bytes 2621440 | tf_op jit(solution)/shard_map/all_to_all | solution.py:146
  24.0 4.4 %collective-permute-start.2 = (bf16[3,1024,256]{2,1,0:T(8,128)(2,1)}, bf16[3,1024,256]{2,1,0:T(8,128)(2,1)S(1)}, u32[]{:S(2)}, u32[]{:S(2)}) collective-permute-start(bf16[3,1024,256]{2,1,0:T(8,128)(2,1)} %get-tuple-element.10.refs_0_), channel_id=1, source_target_pairs={{0,6},{1,7},{2,0},{3,1},{4,2},{5,3},{6,4},{7,5},{8,14},{9,15},{10,... | collective-permute-start | bytes 4718600 | tf_op jit(solution)/shard_map/ppermute | solution.py:108
  28.4 1.9 %collective-permute-start.1 = (bf16[3,1024,256]{2,1,0:T(8,128)(2,1)}, bf16[3,1024,256]{2,1,0:T(8,128)(2,1)S(1)}, u32[]{:S(2)}, u32[]{:S(2)}) collective-permute-start(bf16[3,1024,256]{2,1,0:T(8,128)(2,1)} %get-tuple-element.10.refs_0_), channel_id=1, source_target_pairs={{0,2},{1,3},{2,4},{3,5},{4,6},{5,7},{6,0},{7,1},{8,10},{9,11},{10,... | collective-permute-start | bytes 4718600 | tf_op jit(solution)/shard_map/ppermute | solution.py:108
  30.4 31.2 %collective-permute-done.2.refs_3_ = bf16[3,1024,256]{2,1,0:T(8,128)(2,1)S(1)} collective-permute-done((bf16[3,1024,256]{2,1,0:T(8,128)(2,1)}, bf16[3,1024,256]{2,1,0:T(8,128)(2,1)S(1)}, u32[]{:S(2)}, u32[]{:S(2)}) %collective-permute-start.2) | collective-permute-done | bytes 1572896 | tf_op jit(solution)/shard_map/ppermute | solution.py:108
  61.5 0.0 copy-start
  61.5 5.0 %collective-permute-done.1.refs_2_ = bf16[3,1024,256]{2,1,0:T(8,128)(2,1)S(1)} collective-permute-done((bf16[3,1024,256]{2,1,0:T(8,128)(2,1)}, bf16[3,1024,256]{2,1,0:T(8,128)(2,1)S(1)}, u32[]{:S(2)}, u32[]{:S(2)}) %collective-permute-start.1) | collective-permute-done | bytes 1572896 | tf_op jit(solution)/shard_map/ppermute | solution.py:108
  66.6 0.0 copy-start.1
  66.6 0.2 broadcast_select_fusion
  66.8 1.9 %collective-permute-start.5 = (bf16[3,1024,256]{2,1,0:T(8,128)(2,1)S(1)}, bf16[3,1024,256]{2,1,0:T(8,128)(2,1)S(1)}, u32[]{:S(2)}, u32[]{:S(2)}) collective-permute-start(bf16[3,1024,256]{2,1,0:T(8,128)(2,1)S(1)} %broadcast_select_fusion), channel_id=1, source_target_pairs={{0,2},{1,7},{2,4},{3,1},{4,6},{5,3},{6,0},{7,5},{8,10},{9,15},{10,... | collective-permute-start | bytes 4718600 | tf_op jit(solution)/shard_map/ppermute | solution.py:108
  68.7 3.9 %collective-permute-start = (bf16[3,1024,256]{2,1,0:T(8,128)(2,1)}, bf16[3,1024,256]{2,1,0:T(8,128)(2,1)S(1)}, u32[]{:S(2)}, u32[]{:S(2)}) collective-permute-start(bf16[3,1024,256]{2,1,0:T(8,128)(2,1)} %get-tuple-element.10.refs_0_), channel_id=1, source_target_pairs={{0,1},{1,0},{2,3},{3,2},{4,5},{5,4},{6,7},{7,6},{8,9},{9,8},{10,11... | collective-permute-start | bytes 4718600 | tf_op jit(solution)/shard_map/ppermute | solution.py:111
  72.6 0.0 copy-done
  72.6 1.9 %collective-permute-start.4 = (bf16[3,1024,256]{2,1,0:T(8,128)(2,1)S(1)}, bf16[3,1024,256]{2,1,0:T(8,128)(2,1)S(1)}, u32[]{:S(2)}, u32[]{:S(2)}) collective-permute-start(bf16[3,1024,256]{2,1,0:T(8,128)(2,1)S(1)} %collective-permute-done.2.refs_3_), channel_id=1, source_target_pairs={{0,1},{1,0},{2,3},{3,2},{4,5},{5,4},{6,7},{7,6},{8,9},{9,8},{10,11... | collective-permute-start | bytes 4718600 | tf_op jit(solution)/shard_map/ppermute | solution.py:111
  74.5 0.0 copy-done.1
  74.5 2.4 %collective-permute-start.3 = (bf16[3,1024,256]{2,1,0:T(8,128)(2,1)S(1)}, bf16[3,1024,256]{2,1,0:T(8,128)(2,1)S(1)}, u32[]{:S(2)}, u32[]{:S(2)}) collective-permute-start(bf16[3,1024,256]{2,1,0:T(8,128)(2,1)S(1)} %collective-permute-done.1.refs_2_), channel_id=1, source_target_pairs={{0,1},{1,0},{2,3},{3,2},{4,5},{5,4},{6,7},{7,6},{8,9},{9,8},{10,11... | collective-permute-start | bytes 4718600 | tf_op jit(solution)/shard_map/ppermute | solution.py:111
  76.9 11.4 %collective-permute-done.5.refs_6_ = bf16[3,1024,256]{2,1,0:T(8,128)(2,1)S(1)} collective-permute-done((bf16[3,1024,256]{2,1,0:T(8,128)(2,1)S(1)}, bf16[3,1024,256]{2,1,0:T(8,128)(2,1)S(1)}, u32[]{:S(2)}, u32[]{:S(2)}) %collective-permute-start.5) | collective-permute-done | bytes 1572896 | tf_op jit(solution)/shard_map/ppermute | solution.py:108
  88.3 0.0 copy-start.2
  88.3 6.0 %collective-permute-start.6 = (bf16[3,1024,256]{2,1,0:T(8,128)(2,1)S(1)}, bf16[3,1024,256]{2,1,0:T(8,128)(2,1)}, u32[]{:S(2)}, u32[]{:S(2)}) collective-permute-start(bf16[3,1024,256]{2,1,0:T(8,128)(2,1)S(1)} %collective-permute-done.5.refs_6_), channel_id=1, source_target_pairs={{0,1},{1,0},{2,3},{3,2},{4,5},{5,4},{6,7},{7,6},{8,9},{9,8},{10,11... | collective-permute-start | bytes 4718600 | tf_op jit(solution)/shard_map/ppermute | solution.py:111
  94.3 0.0 collective-permute-done.refs_1_
  94.4 0.0 copy-start.3
  94.4 0.0 collective-permute-done.4.refs_5_
  94.4 0.0 copy-start.4
  94.4 0.0 collective-permute-done.3.refs_4_
  94.4 0.0 copy-done.2
  94.4 1.1 copy-done.3
  95.5 0.6 copy-done.4
  96.1 0.0 copy-start.5
  96.1 1.1 copy-done.5
  97.3 0.1 collective-permute-done.6.refs_7_
  97.3 0.0 all-to-all-done
  97.3 0.0 copy-start.6
  97.3 16.6 %expert_grad.1 = bf16[2560,128]{1,0:T(8,128)(2,1)} custom-call(bf16[5120,128]{1,0:T(8,128)(2,1)} %bitcast.3.rows_ref, bf16[3,1024,256]{2,1,0:T(8,128)(2,1)} %get-tuple-element.10.refs_0_, bf16[3,1024,256]{2,1,0:T(8,128)(2,1)} %copy-done.3, bf16[3,1024,256]{2,1,0:T(8,128)(2,1)} %copy-done.1, bf16[3,1024,256]{2,1,0:T(8,128)(2,1)} %copy-done, ...), custom_call_target="tpu_custom_call" | custom-call | tf_op jit(solution)/shard_map/expert_grad/pallas_call | solution.py:148
  113.9 49.6 %all_to_all.16 = bf16[320,8,128]{2,1,0:T(8,128)(2,1)S(1)} all-to-all(bf16[320,8,128]{2,1,0:T(8,128)(2,1)} %bitcast.10), channel_id=1, replica_groups=mesh['expert'=64,'tensor'=8] {'expert'}, dimensions={0} | all-to-all | bytes 1310720 | tf_op jit(solution)/shard_map/all_to_all | solution.py:165
  163.6 0.0 copy-done.6
  163.6 1.0 convolution_convert_fusion
Async XLA Ops:
  4.5 92.8 %all-to-all-start = ((bf16[64,80,128]{2,1,0:T(8,128)(2,1)}), bf16[64,80,128]{2,1,0:T(8,128)(2,1)}, u32[]{:S(2)}, u32[]{:S(2)}) async-start(bf16[64,80,128]{2,1,0:T(8,128)(2,1)} %bitcast.12), calls=%async_computation | async-start | bytes 2621440 | tf_op jit(solution)/shard_map/all_to_all | solution.py:146
  24.0 37.5 %collective-permute-start.2 = (bf16[3,1024,256]{2,1,0:T(8,128)(2,1)}, bf16[3,1024,256]{2,1,0:T(8,128)(2,1)S(1)}, u32[]{:S(2)}, u32[]{:S(2)}) collective-permute-start(bf16[3,1024,256]{2,1,0:T(8,128)(2,1)} %get-tuple-element.10.refs_0_), channel_id=1, source_target_pairs={{0,6},{1,7},{2,0},{3,1},{4,2},{5,3},{6,4},{7,5},{8,14},{9,15},{10,... | collective-permute-start | bytes 4718600 | tf_op jit(solution)/shard_map/ppermute | solution.py:108
  28.4 38.1 %collective-permute-start.1 = (bf16[3,1024,256]{2,1,0:T(8,128)(2,1)}, bf16[3,1024,256]{2,1,0:T(8,128)(2,1)S(1)}, u32[]{:S(2)}, u32[]{:S(2)}) collective-permute-start(bf16[3,1024,256]{2,1,0:T(8,128)(2,1)} %get-tuple-element.10.refs_0_), channel_id=1, source_target_pairs={{0,2},{1,3},{2,4},{3,5},{4,6},{5,7},{6,0},{7,1},{8,10},{9,11},{10,... | collective-permute-start | bytes 4718600 | tf_op jit(solution)/shard_map/ppermute | solution.py:108
  61.5 11.0 %copy-start = (bf16[3,1024,256]{2,1,0:T(8,128)(2,1)}, bf16[3,1024,256]{2,1,0:T(8,128)(2,1)S(1)}, u32[]{:S(2)}) copy-start(bf16[3,1024,256]{2,1,0:T(8,128)(2,1)S(1)} %collective-permute-done.2.refs_3_) | copy-start | bytes 4718596
  66.6 7.9 %copy-start.1 = (bf16[3,1024,256]{2,1,0:T(8,128)(2,1)}, bf16[3,1024,256]{2,1,0:T(8,128)(2,1)S(1)}, u32[]{:S(2)}) copy-start(bf16[3,1024,256]{2,1,0:T(8,128)(2,1)S(1)} %collective-permute-done.1.refs_2_) | copy-start | bytes 4718596
  66.8 21.6 %collective-permute-start.5 = (bf16[3,1024,256]{2,1,0:T(8,128)(2,1)S(1)}, bf16[3,1024,256]{2,1,0:T(8,128)(2,1)S(1)}, u32[]{:S(2)}, u32[]{:S(2)}) collective-permute-start(bf16[3,1024,256]{2,1,0:T(8,128)(2,1)S(1)} %broadcast_select_fusion), channel_id=1, source_target_pairs={{0,2},{1,7},{2,4},{3,1},{4,6},{5,3},{6,0},{7,5},{8,10},{9,15},{10,... | collective-permute-start | bytes 4718600 | tf_op jit(solution)/shard_map/ppermute | solution.py:108
  68.7 25.7 %collective-permute-start = (bf16[3,1024,256]{2,1,0:T(8,128)(2,1)}, bf16[3,1024,256]{2,1,0:T(8,128)(2,1)S(1)}, u32[]{:S(2)}, u32[]{:S(2)}) collective-permute-start(bf16[3,1024,256]{2,1,0:T(8,128)(2,1)} %get-tuple-element.10.refs_0_), channel_id=1, source_target_pairs={{0,1},{1,0},{2,3},{3,2},{4,5},{5,4},{6,7},{7,6},{8,9},{9,8},{10,11... | collective-permute-start | bytes 4718600 | tf_op jit(solution)/shard_map/ppermute | solution.py:111
  72.6 21.8 %collective-permute-start.4 = (bf16[3,1024,256]{2,1,0:T(8,128)(2,1)S(1)}, bf16[3,1024,256]{2,1,0:T(8,128)(2,1)S(1)}, u32[]{:S(2)}, u32[]{:S(2)}) collective-permute-start(bf16[3,1024,256]{2,1,0:T(8,128)(2,1)S(1)} %collective-permute-done.2.refs_3_), channel_id=1, source_target_pairs={{0,1},{1,0},{2,3},{3,2},{4,5},{5,4},{6,7},{7,6},{8,9},{9,8},{10,11... | collective-permute-start | bytes 4718600 | tf_op jit(solution)/shard_map/ppermute | solution.py:111
  74.5 19.9 %collective-permute-start.3 = (bf16[3,1024,256]{2,1,0:T(8,128)(2,1)S(1)}, bf16[3,1024,256]{2,1,0:T(8,128)(2,1)S(1)}, u32[]{:S(2)}, u32[]{:S(2)}) collective-permute-start(bf16[3,1024,256]{2,1,0:T(8,128)(2,1)S(1)} %collective-permute-done.1.refs_2_), channel_id=1, source_target_pairs={{0,1},{1,0},{2,3},{3,2},{4,5},{5,4},{6,7},{7,6},{8,9},{9,8},{10,11... | collective-permute-start | bytes 4718600 | tf_op jit(solution)/shard_map/ppermute | solution.py:111
  88.3 6.1 %copy-start.2 = (bf16[3,1024,256]{2,1,0:T(8,128)(2,1)}, bf16[3,1024,256]{2,1,0:T(8,128)(2,1)S(1)}, u32[]{:S(2)}) copy-start(bf16[3,1024,256]{2,1,0:T(8,128)(2,1)S(1)} %collective-permute-done.5.refs_6_) | copy-start | bytes 4718596
  88.3 9.0 %collective-permute-start.6 = (bf16[3,1024,256]{2,1,0:T(8,128)(2,1)S(1)}, bf16[3,1024,256]{2,1,0:T(8,128)(2,1)}, u32[]{:S(2)}, u32[]{:S(2)}) collective-permute-start(bf16[3,1024,256]{2,1,0:T(8,128)(2,1)S(1)} %collective-permute-done.5.refs_6_), channel_id=1, source_target_pairs={{0,1},{1,0},{2,3},{3,2},{4,5},{5,4},{6,7},{7,6},{8,9},{9,8},{10,11... | collective-permute-start | bytes 4718600 | tf_op jit(solution)/shard_map/ppermute | solution.py:111
  94.4 1.1 copy-start.3
  94.4 1.7 %copy-start.4 = (bf16[3,1024,256]{2,1,0:T(8,128)(2,1)}, bf16[3,1024,256]{2,1,0:T(8,128)(2,1)S(1)}, u32[]{:S(2)}) copy-start(bf16[3,1024,256]{2,1,0:T(8,128)(2,1)S(1)} %collective-permute-done.4.refs_5_) | copy-start | bytes 4718596
  96.1 1.1 copy-start.5
  97.3 66.3 %copy-start.6 = (bf16[320,128]{1,0:T(8,128)(2,1)S(1)}, bf16[320,128]{1,0:T(8,128)(2,1)}, u32[]{:S(2)}) copy-start(bf16[320,128]{1,0:T(8,128)(2,1)} %get-tuple-element.8) | copy-start | bytes 245764

commit v5 on v4

v5 whole, which is shorter than its diff:
```python
import jax
import jax.numpy as jnp
from jax import lax
from jax.experimental import pallas as pl
from jax.experimental.pallas import tpu as pltpu
from jax.sharding import PartitionSpec as P


level_scale = 1.0 / 256.0
vmem_limit = 56 * 1024 * 1024
groups = 8
chunks = 4
pair = 2


def route_kernel(capacity, experts, *refs):
    tok_ref, grad_ref, ids_ref, lev_ref, gate_ref, up_ref, down_ref = refs[:7]
    send_ref, comb_ref, stack_ref, stage_ref, buf_ref, sems = refs[7:]
    weights = (gate_ref, up_ref, down_ref)
    loads = [pltpu.make_async_copy(ref.at[0], buf_ref.at[i], sems.at[0, i]) for i, ref in enumerate(weights)]
    stores = [pltpu.make_async_copy(buf_ref.at[i], stack_ref.at[i], sems.at[1, i]) for i in range(3)]
    for load in loads:
        load.start()
    count = ids_ref.shape[1]
    slots = comb_ref.shape[0]
    ids0 = ids_ref[0:1, :]
    ids1 = ids_ref[1:2, :]
    lane_e = lax.broadcasted_iota(jnp.int32, (experts, count), 0)
    hot0 = (lane_e == ids0).astype(jnp.float32)
    hot1 = (lane_e == ids1).astype(jnp.float32)
    row_i = lax.broadcasted_iota(jnp.int32, (count, count), 0)
    col_i = lax.broadcasted_iota(jnp.int32, (count, count), 1)
    upper = (row_i <= col_i).astype(jnp.bfloat16)
    run0 = jnp.dot(hot0.astype(jnp.bfloat16), upper, preferred_element_type=jnp.float32)
    run1 = jnp.dot(hot1.astype(jnp.bfloat16), upper, preferred_element_type=jnp.float32)
    run1 = run1 + jnp.sum(hot0, axis=1, keepdims=True)
    rank0 = jnp.sum(hot0 * run0, axis=0, keepdims=True).astype(jnp.int32) - 1
    rank1 = jnp.sum(hot1 * run1, axis=0, keepdims=True).astype(jnp.int32) - 1
    slot0 = ids0 * capacity + rank0
    slot1 = ids1 * capacity + rank1
    slot_i = lax.broadcasted_iota(jnp.int32, (slots, count), 0)
    at0 = slot_i == slot0
    at1 = slot_i == slot1
    scale = lev_ref[...].astype(jnp.float32) * level_scale
    comb = jnp.where(at0, scale[0:1, :], 0.0) + jnp.where(at1, scale[1:2, :], 0.0)
    comb_ref[...] = comb.astype(jnp.bfloat16)
    pick = jnp.where(at0 | at1, 1.0, 0.0).astype(jnp.bfloat16)
    for load, store in zip(loads, stores):
        load.wait()
        store.start()
    for half, source in enumerate((tok_ref, grad_ref)):
        rows = jnp.dot(pick, source[...], preferred_element_type=jnp.float32)
        for c in range(groups):
            stage_ref[pl.ds(half * groups + c, slots, stride=2 * groups), :] = rows[:, c * 128:(c + 1) * 128]
    send_ref[...] = stage_ref[...].astype(jnp.bfloat16)
    for store in stores:
        store.wait()


def call_route(capacity, experts, tokens, out_grad, ids, levels, weights):
    tok_count, width = tokens.shape
    slots = experts * capacity
    stack_shape = (3,) + weights[0].shape[1:]
    tall = (slots * 2 * groups, width // groups)
    vmem = pl.BlockSpec(memory_space=pltpu.VMEM)
    hbm = pl.BlockSpec(memory_space=pl.ANY)
    return pl.pallas_call(
        lambda *refs: route_kernel(capacity, experts, *refs),
        name="route",
        out_shape=(
            jax.ShapeDtypeStruct(tall, jnp.bfloat16),
            jax.ShapeDtypeStruct((slots, tok_count), jnp.bfloat16),
            jax.ShapeDtypeStruct(stack_shape, jnp.bfloat16),
        ),
        in_specs=[vmem] * 4 + [hbm] * 3,
        out_specs=(vmem, vmem, hbm),
        scratch_shapes=[
            pltpu.VMEM(tall, jnp.float32),
            pltpu.VMEM(stack_shape, jnp.bfloat16),
            pltpu.SemaphoreType.DMA((2, 3)),
        ],
        compiler_params=pltpu.CompilerParams(vmem_limit_bytes=vmem_limit),
    )(tokens, out_grad, ids, levels, *weights)


def expert_kernel(rows_hbm, *refs):
    count = len(refs) - 11
    weights = refs[:count]
    out_hbm, acc_ref, buf_ref, rows_ref, stage_ref, tok_ref, grad_ref, out_ref, sems, in_sems, out_sems = refs[count:]
    slots = acc_ref.shape[0]
    rows_per = slots // chunks
    tall = rows_per * 2 * groups
    short = rows_per * groups

    def fetch(block):
        return [pltpu.make_async_copy(weights[block].at[i], buf_ref.at[block, i], sems.at[block, i]) for i in range(3)]

    arrivals = []
    for q in range(chunks):
        part = pl.ds(q * tall, tall)
        arrivals.append(pltpu.make_async_copy(rows_hbm.at[part], rows_ref.at[part], in_sems.at[q]))
        arrivals[-1].start()
    copies = [fetch(block) for block in range(count)]
    for block in range(pair):
        for copy in copies[block]:
            copy.start()
    for q in range(chunks):
        arrivals[q].wait()
        part = pl.ds(q * tall, tall)
        stage_ref[part, :] = rows_ref[part, :].astype(jnp.float32)
        for half, target in enumerate((tok_ref, grad_ref)):
            for c in range(groups):
                piece = stage_ref[pl.ds(q * tall + half * groups + c, rows_per, stride=2 * groups), :]
                target[q * rows_per:(q + 1) * rows_per, c * 128:(c + 1) * 128] = piece.astype(jnp.bfloat16)
    for block in range(pair, count):
        for copy in copies[block]:
            copy.start()
    back = (((1,), (1,)), ((), ()))
    for first in range(0, count, pair):
        lefts = []
        rights = []
        for block in range(first, first + pair):
            for copy in copies[block]:
                copy.wait()
        for block in range(first, first + pair):
            gate_cols = buf_ref[block, 0]
            up_cols = buf_ref[block, 1]
            down_cols = buf_ref[block, 2]
            gate_pre = jnp.dot(tok_ref[...], gate_cols, preferred_element_type=jnp.float32)
            up_pre = jnp.dot(tok_ref[...], up_cols, preferred_element_type=jnp.float32)
            hidden_grad = jnp.dot(grad_ref[...], down_cols, preferred_element_type=jnp.float32)
            sig = jax.nn.sigmoid(gate_pre)
            up_grad = (hidden_grad * gate_pre * sig).astype(jnp.bfloat16)
            gate_grad = (hidden_grad * up_pre * sig * (1.0 + gate_pre * (1.0 - sig))).astype(jnp.bfloat16)
            lefts += [gate_grad, up_grad]
            rights += [gate_cols, up_cols]
        part = lax.dot_general(
            jnp.concatenate(lefts, 1), jnp.concatenate(rights, 1), back, preferred_element_type=jnp.float32
        )
        if first == 0:
            acc_ref[...] = part
        elif first + pair < count:
            acc_ref[...] = acc_ref[...] + part
        else:
            part = acc_ref[...] + part
            for c in range(groups):
                stage_ref[pl.ds(c, slots, stride=groups), :] = part[:, c * 128:(c + 1) * 128]
    leaves = []
    for q in range(chunks):
        part = pl.ds(q * short, short)
        out_ref[part, :] = stage_ref[part, :].astype(jnp.bfloat16)
        leaves.append(pltpu.make_async_copy(out_ref.at[part], out_hbm.at[part], out_sems.at[q]))
        leaves[-1].start()
    for copy in leaves:
        copy.wait()


def call_expert(rows, blocks):
    tall, lanes = rows.shape
    slots = tall // (2 * groups)
    width = lanes * groups
    hbm = pl.BlockSpec(memory_space=pl.ANY)
    short = (slots * groups, lanes)
    return pl.pallas_call(
        expert_kernel,
        name="expert_grad",
        out_shape=jax.ShapeDtypeStruct(short, jnp.bfloat16),
        in_specs=[hbm] * (1 + len(blocks)),
        out_specs=hbm,
        scratch_shapes=[
            pltpu.VMEM((slots, width), jnp.float32),
            pltpu.VMEM((len(blocks),) + blocks[0].shape, jnp.bfloat16),
            pltpu.VMEM((tall, lanes), jnp.bfloat16),
            pltpu.VMEM((tall, lanes), jnp.float32),
            pltpu.VMEM((slots, width), jnp.bfloat16),
            pltpu.VMEM((slots, width), jnp.bfloat16),
            pltpu.VMEM(short, jnp.bfloat16),
            pltpu.SemaphoreType.DMA((len(blocks), 3)),
            pltpu.SemaphoreType.DMA((chunks,)),
            pltpu.SemaphoreType.DMA((chunks,)),
        ],
        compiler_params=pltpu.CompilerParams(vmem_limit_bytes=vmem_limit),
    )(rows, *blocks)


def gather_weights(weights):
    core = lax.axis_index("tensor") % 2
    chips = lax.axis_size("tensor") // 2

    def shift(value, step0, step1):
        pairs = []
        for chip in range(chips):
            pairs.append((2 * chip, 2 * ((chip + step0) % chips)))
            pairs.append((2 * chip + 1, 2 * ((chip + step1) % chips) + 1))
        return lax.ppermute(value, "tensor", pairs)

    def swap(value):
        return lax.ppermute(value, "tensor", [(i, i ^ 1) for i in range(2 * chips)])

    left = shift(weights, 1, 1)
    right = shift(weights, -1, -1)
    far = shift(jnp.where(core == 0, left, right), 1, -1)
    return [weights, swap(weights), left, right, swap(left), swap(right), far, swap(far)]


def on_device(tokens, out_grad, expert_ids, gate_levels, gate_weight, up_weight, down_weight):
    _, width = tokens.shape
    experts = lax.axis_size("expert")
    capacity = 5
    slots = experts * capacity
    lanes = width // groups
    stacked = (gate_weight, up_weight, down_weight)
    send, comb, weights = call_route(
        capacity, experts, tokens, out_grad, expert_ids.T, gate_levels.T, stacked
    )
    received = lax.all_to_all(send, "expert", split_axis=0, concat_axis=0, tiled=True)
    blocks = gather_weights(weights)
    result = call_expert(received, blocks)
    result = result.reshape(slots, groups, lanes)
    returned = lax.all_to_all(result, "expert", split_axis=0, concat_axis=0, tiled=True)
    returned = returned.reshape(slots, width)
    total = lax.dot_general(comb, returned, (((0,), (0,)), ((), ())), preferred_element_type=jnp.float32)
    return total.astype(jnp.bfloat16)


def solution(mesh):
    return jax.shard_map(
        on_device,
        mesh=mesh,
        in_specs=(
            P(("expert", "tensor"), None),
            P(("expert", "tensor"), None),
            P(("expert", "tensor"), None),
            P(("expert", "tensor"), None),
            P("expert", None, "tensor"),
            P("expert", None, "tensor"),
            P("expert", None, "tensor"),
        ),
        out_specs=P(("expert", "tensor"), None),
        check_vma=False,
    )
```

time: 167 us -> 161 us (0.964)
  Pallas kernels: 21.1 us -> 15.7 us
    pallas_call x2, Pallas kernels: 21.1 us -> 15.7 us  [the longest x1 11.2 us: call_expert(): pl.pallas_call(expert_kernel, name='expert_grad', out_shape=jax.ShapeDtyp...]
where the time goes in v5:
time: 161 us; the launch traced here: 159 us
  blocking collectives  49.7 us (31%)
  waiting for transfers between devices  47.8 us (30%)
  starting transfers between devices  41.8 us (26%)
  Pallas kernels  15.7 us (10%)
  local copies, waits for them, and re-layouts  2.86 us (2%)
    all_to_all x1, blocking collectives, on_device(): lax.all_to_all(result, 'expert', split_axis=0, concat_axis=0, tiled=True)  49.7 us
    ppermute x3, waiting for transfers between devices, shift(): return lax.ppermute(value, 'tensor', pairs)  47.5 us
    all_to_all x1, starting transfers between devices, on_device(): lax.all_to_all(send, 'expert', split_axis=0, concat_axis=0, tiled=True)  19.5 us
    ppermute x4, starting transfers between devices, swap(): return lax.ppermute(value, 'tensor', [(i, i ^ 1) for i in range(2 * chips)])  14.1 us
    pallas_call x1, Pallas kernels, call_expert(): pl.pallas_call(expert_kernel, name='expert_grad', out_shape=jax.ShapeDtyp...  11.2 us
    ppermute x3, starting transfers between devices, shift(): return lax.ppermute(value, 'tensor', pairs)  8.22 us
    pallas_call x1, Pallas kernels, call_route(): pl.pallas_call(lambda *refs: route_kernel(capacity, experts, *refs), name...  4.52 us
  transfers between devices with their start and end apart: 8, of which 4 were waited for; matrix products, arithmetic and copies ran while one was open for 0% of the time, Pallas kernels for 0%

profile of v5, /device:TPU:1, one launch (start us, length us, event | category | flops | bytes accessed | tf_op | source)
XLA Modules:
  0.0 159.2 jit_solution(17981884335344142575)
XLA Ops:
  0.0 4.5 %route.1 = (bf16[5120,128]{1,0:T(8,128)(2,1)}, bf16[320,128]{1,0:T(8,128)(2,1)}, bf16[3,1024,256]{2,1,0:T(8,128)(2,1)}) custom-call(bf16[128,1024]{1,0:T(8,128)(2,1)} %refs_0_.1, bf16[128,1024]{1,0:T(8,128)(2,1)} %refs_1_.1, s32[2,128]{1,0:T(2,128)} %bitcast.13, s32[2,128]{1,0:T(2,128)} %bitcast.14, bf16[1,1024,256]{2,1,0:T(8,128)(2,1)} %refs_4_.1, ...), custom_call_target="tpu_custom_call" | custom-call | tf_op jit(solution)/shard_map/route/pallas_call | solution.py:67
  4.5 19.5 %all-to-all-start = ((bf16[64,80,128]{2,1,0:T(8,128)(2,1)}), bf16[64,80,128]{2,1,0:T(8,128)(2,1)}, u32[]{:S(2)}, u32[]{:S(2)}) async-start(bf16[64,80,128]{2,1,0:T(8,128)(2,1)} %bitcast.12), calls=%async_computation | async-start | bytes 2621440 | tf_op jit(solution)/shard_map/all_to_all | solution.py:216
  24.1 4.4 %collective-permute-start.2 = (bf16[3,1024,256]{2,1,0:T(8,128)(2,1)}, bf16[3,1024,256]{2,1,0:T(8,128)(2,1)S(1)}, u32[]{:S(2)}, u32[]{:S(2)}) collective-permute-start(bf16[3,1024,256]{2,1,0:T(8,128)(2,1)} %get-tuple-element.10.refs_0_), channel_id=1, source_target_pairs={{0,6},{1,7},{2,0},{3,1},{4,2},{5,3},{6,4},{7,5},{8,14},{9,15},{10,... | collective-permute-start | bytes 4718600 | tf_op jit(solution)/shard_map/ppermute | solution.py:195
  28.4 1.9 %collective-permute-start.1 = (bf16[3,1024,256]{2,1,0:T(8,128)(2,1)}, bf16[3,1024,256]{2,1,0:T(8,128)(2,1)S(1)}, u32[]{:S(2)}, u32[]{:S(2)}) collective-permute-start(bf16[3,1024,256]{2,1,0:T(8,128)(2,1)} %get-tuple-element.10.refs_0_), channel_id=1, source_target_pairs={{0,2},{1,3},{2,4},{3,5},{4,6},{5,7},{6,0},{7,1},{8,10},{9,11},{10,... | collective-permute-start | bytes 4718600 | tf_op jit(solution)/shard_map/ppermute | solution.py:195
  30.4 31.1 %collective-permute-done.2.refs_3_ = bf16[3,1024,256]{2,1,0:T(8,128)(2,1)S(1)} collective-permute-done((bf16[3,1024,256]{2,1,0:T(8,128)(2,1)}, bf16[3,1024,256]{2,1,0:T(8,128)(2,1)S(1)}, u32[]{:S(2)}, u32[]{:S(2)}) %collective-permute-start.2) | collective-permute-done | bytes 1572896 | tf_op jit(solution)/shard_map/ppermute | solution.py:195
  61.5 0.0 copy-start
  61.5 5.0 %collective-permute-done.1.refs_2_ = bf16[3,1024,256]{2,1,0:T(8,128)(2,1)S(1)} collective-permute-done((bf16[3,1024,256]{2,1,0:T(8,128)(2,1)}, bf16[3,1024,256]{2,1,0:T(8,128)(2,1)S(1)}, u32[]{:S(2)}, u32[]{:S(2)}) %collective-permute-start.1) | collective-permute-done | bytes 1572896 | tf_op jit(solution)/shard_map/ppermute | solution.py:195
  66.6 0.0 copy-start.1
  66.6 0.2 broadcast_select_fusion
  66.7 1.9 %collective-permute-start.5 = (bf16[3,1024,256]{2,1,0:T(8,128)(2,1)S(1)}, bf16[3,1024,256]{2,1,0:T(8,128)(2,1)S(1)}, u32[]{:S(2)}, u32[]{:S(2)}) collective-permute-start(bf16[3,1024,256]{2,1,0:T(8,128)(2,1)S(1)} %broadcast_select_fusion), channel_id=1, source_target_pairs={{0,2},{1,7},{2,4},{3,1},{4,6},{5,3},{6,0},{7,5},{8,10},{9,15},{10,... | collective-permute-start | bytes 4718600 | tf_op jit(solution)/shard_map/ppermute | solution.py:195
  68.7 3.9 %collective-permute-start = (bf16[3,1024,256]{2,1,0:T(8,128)(2,1)}, bf16[3,1024,256]{2,1,0:T(8,128)(2,1)S(1)}, u32[]{:S(2)}, u32[]{:S(2)}) collective-permute-start(bf16[3,1024,256]{2,1,0:T(8,128)(2,1)} %get-tuple-element.10.refs_0_), channel_id=1, source_target_pairs={{0,1},{1,0},{2,3},{3,2},{4,5},{5,4},{6,7},{7,6},{8,9},{9,8},{10,11... | collective-permute-start | bytes 4718600 | tf_op jit(solution)/shard_map/ppermute | solution.py:198
  72.6 0.0 copy-done
  72.6 1.9 %collective-permute-start.4 = (bf16[3,1024,256]{2,1,0:T(8,128)(2,1)S(1)}, bf16[3,1024,256]{2,1,0:T(8,128)(2,1)S(1)}, u32[]{:S(2)}, u32[]{:S(2)}) collective-permute-start(bf16[3,1024,256]{2,1,0:T(8,128)(2,1)S(1)} %collective-permute-done.2.refs_3_), channel_id=1, source_target_pairs={{0,1},{1,0},{2,3},{3,2},{4,5},{5,4},{6,7},{7,6},{8,9},{9,8},{10,11... | collective-permute-start | bytes 4718600 | tf_op jit(solution)/shard_map/ppermute | solution.py:198
  74.5 0.0 copy-done.1
  74.5 2.4 %collective-permute-start.3 = (bf16[3,1024,256]{2,1,0:T(8,128)(2,1)S(1)}, bf16[3,1024,256]{2,1,0:T(8,128)(2,1)S(1)}, u32[]{:S(2)}, u32[]{:S(2)}) collective-permute-start(bf16[3,1024,256]{2,1,0:T(8,128)(2,1)S(1)} %collective-permute-done.1.refs_2_), channel_id=1, source_target_pairs={{0,1},{1,0},{2,3},{3,2},{4,5},{5,4},{6,7},{7,6},{8,9},{9,8},{10,11... | collective-permute-start | bytes 4718600 | tf_op jit(solution)/shard_map/ppermute | solution.py:198
  76.9 11.4 %collective-permute-done.5.refs_6_ = bf16[3,1024,256]{2,1,0:T(8,128)(2,1)S(1)} collective-permute-done((bf16[3,1024,256]{2,1,0:T(8,128)(2,1)S(1)}, bf16[3,1024,256]{2,1,0:T(8,128)(2,1)S(1)}, u32[]{:S(2)}, u32[]{:S(2)}) %collective-permute-start.5) | collective-permute-done | bytes 1572896 | tf_op jit(solution)/shard_map/ppermute | solution.py:195
  88.3 0.0 copy-start.2
  88.3 5.9 %collective-permute-start.6 = (bf16[3,1024,256]{2,1,0:T(8,128)(2,1)S(1)}, bf16[3,1024,256]{2,1,0:T(8,128)(2,1)}, u32[]{:S(2)}, u32[]{:S(2)}) collective-permute-start(bf16[3,1024,256]{2,1,0:T(8,128)(2,1)S(1)} %collective-permute-done.5.refs_6_), channel_id=1, source_target_pairs={{0,1},{1,0},{2,3},{3,2},{4,5},{5,4},{6,7},{7,6},{8,9},{9,8},{10,11... | collective-permute-start | bytes 4718600 | tf_op jit(solution)/shard_map/ppermute | solution.py:198
  94.2 0.0 collective-permute-done.refs_1_
  94.2 0.0 copy-start.3
  94.2 0.0 collective-permute-done.4.refs_5_
  94.2 0.0 copy-start.4
  94.2 0.0 collective-permute-done.3.refs_4_
  94.2 0.0 copy-done.2
  94.2 1.1 copy-done.3
  95.3 0.6 copy-done.4
  95.9 0.0 copy-start.5
  95.9 1.1 copy-done.5
  97.1 0.2 collective-permute-done.6.refs_7_
  97.3 0.0 all-to-all-done
  97.3 0.0 copy-start.6
  97.3 11.2 %expert_grad.1 = bf16[2560,128]{1,0:T(8,128)(2,1)} custom-call(bf16[5120,128]{1,0:T(8,128)(2,1)} %bitcast.3.rows_hbm, bf16[3,1024,256]{2,1,0:T(8,128)(2,1)} %get-tuple-element.10.refs_0_, bf16[3,1024,256]{2,1,0:T(8,128)(2,1)} %copy-done.3, bf16[3,1024,256]{2,1,0:T(8,128)(2,1)} %copy-done.1, bf16[3,1024,256]{2,1,0:T(8,128)(2,1)} %copy-done, ...), custom_call_target="tpu_custom_call" | custom-call | tf_op jit(solution)/shard_map/expert_grad/pallas_call | solution.py:164
  108.5 49.7 %all_to_all.16 = bf16[320,8,128]{2,1,0:T(8,128)(2,1)S(1)} all-to-all(bf16[320,8,128]{2,1,0:T(8,128)(2,1)} %bitcast.10), channel_id=1, replica_groups=mesh['expert'=64,'tensor'=8] {'expert'}, dimensions={0} | all-to-all | bytes 1310720 | tf_op jit(solution)/shard_map/all_to_all | solution.py:220
  158.2 0.0 copy-done.6
  158.2 1.0 convolution_convert_fusion
Async XLA Ops:
  4.5 92.8 %all-to-all-start = ((bf16[64,80,128]{2,1,0:T(8,128)(2,1)}), bf16[64,80,128]{2,1,0:T(8,128)(2,1)}, u32[]{:S(2)}, u32[]{:S(2)}) async-start(bf16[64,80,128]{2,1,0:T(8,128)(2,1)} %bitcast.12), calls=%async_computation | async-start | bytes 2621440 | tf_op jit(solution)/shard_map/all_to_all | solution.py:216
  24.1 37.5 %collective-permute-start.2 = (bf16[3,1024,256]{2,1,0:T(8,128)(2,1)}, bf16[3,1024,256]{2,1,0:T(8,128)(2,1)S(1)}, u32[]{:S(2)}, u32[]{:S(2)}) collective-permute-start(bf16[3,1024,256]{2,1,0:T(8,128)(2,1)} %get-tuple-element.10.refs_0_), channel_id=1, source_target_pairs={{0,6},{1,7},{2,0},{3,1},{4,2},{5,3},{6,4},{7,5},{8,14},{9,15},{10,... | collective-permute-start | bytes 4718600 | tf_op jit(solution)/shard_map/ppermute | solution.py:195
  28.4 38.1 %collective-permute-start.1 = (bf16[3,1024,256]{2,1,0:T(8,128)(2,1)}, bf16[3,1024,256]{2,1,0:T(8,128)(2,1)S(1)}, u32[]{:S(2)}, u32[]{:S(2)}) collective-permute-start(bf16[3,1024,256]{2,1,0:T(8,128)(2,1)} %get-tuple-element.10.refs_0_), channel_id=1, source_target_pairs={{0,2},{1,3},{2,4},{3,5},{4,6},{5,7},{6,0},{7,1},{8,10},{9,11},{10,... | collective-permute-start | bytes 4718600 | tf_op jit(solution)/shard_map/ppermute | solution.py:195
  61.5 11.1 %copy-start = (bf16[3,1024,256]{2,1,0:T(8,128)(2,1)}, bf16[3,1024,256]{2,1,0:T(8,128)(2,1)S(1)}, u32[]{:S(2)}) copy-start(bf16[3,1024,256]{2,1,0:T(8,128)(2,1)S(1)} %collective-permute-done.2.refs_3_) | copy-start | bytes 4718596
  66.6 7.9 %copy-start.1 = (bf16[3,1024,256]{2,1,0:T(8,128)(2,1)}, bf16[3,1024,256]{2,1,0:T(8,128)(2,1)S(1)}, u32[]{:S(2)}) copy-start(bf16[3,1024,256]{2,1,0:T(8,128)(2,1)S(1)} %collective-permute-done.1.refs_2_) | copy-start | bytes 4718596
  66.7 21.6 %collective-permute-start.5 = (bf16[3,1024,256]{2,1,0:T(8,128)(2,1)S(1)}, bf16[3,1024,256]{2,1,0:T(8,128)(2,1)S(1)}, u32[]{:S(2)}, u32[]{:S(2)}) collective-permute-start(bf16[3,1024,256]{2,1,0:T(8,128)(2,1)S(1)} %broadcast_select_fusion), channel_id=1, source_target_pairs={{0,2},{1,7},{2,4},{3,1},{4,6},{5,3},{6,0},{7,5},{8,10},{9,15},{10,... | collective-permute-start | bytes 4718600 | tf_op jit(solution)/shard_map/ppermute | solution.py:195
  68.7 25.5 %collective-permute-start = (bf16[3,1024,256]{2,1,0:T(8,128)(2,1)}, bf16[3,1024,256]{2,1,0:T(8,128)(2,1)S(1)}, u32[]{:S(2)}, u32[]{:S(2)}) collective-permute-start(bf16[3,1024,256]{2,1,0:T(8,128)(2,1)} %get-tuple-element.10.refs_0_), channel_id=1, source_target_pairs={{0,1},{1,0},{2,3},{3,2},{4,5},{5,4},{6,7},{7,6},{8,9},{9,8},{10,11... | collective-permute-start | bytes 4718600 | tf_op jit(solution)/shard_map/ppermute | solution.py:198
  72.6 21.6 %collective-permute-start.4 = (bf16[3,1024,256]{2,1,0:T(8,128)(2,1)S(1)}, bf16[3,1024,256]{2,1,0:T(8,128)(2,1)S(1)}, u32[]{:S(2)}, u32[]{:S(2)}) collective-permute-start(bf16[3,1024,256]{2,1,0:T(8,128)(2,1)S(1)} %collective-permute-done.2.refs_3_), channel_id=1, source_target_pairs={{0,1},{1,0},{2,3},{3,2},{4,5},{5,4},{6,7},{7,6},{8,9},{9,8},{10,11... | collective-permute-start | bytes 4718600 | tf_op jit(solution)/shard_map/ppermute | solution.py:198
  74.5 19.7 %collective-permute-start.3 = (bf16[3,1024,256]{2,1,0:T(8,128)(2,1)S(1)}, bf16[3,1024,256]{2,1,0:T(8,128)(2,1)S(1)}, u32[]{:S(2)}, u32[]{:S(2)}) collective-permute-start(bf16[3,1024,256]{2,1,0:T(8,128)(2,1)S(1)} %collective-permute-done.1.refs_2_), channel_id=1, source_target_pairs={{0,1},{1,0},{2,3},{3,2},{4,5},{5,4},{6,7},{7,6},{8,9},{9,8},{10,11... | collective-permute-start | bytes 4718600 | tf_op jit(solution)/shard_map/ppermute | solution.py:198
  88.3 5.9 %copy-start.2 = (bf16[3,1024,256]{2,1,0:T(8,128)(2,1)}, bf16[3,1024,256]{2,1,0:T(8,128)(2,1)S(1)}, u32[]{:S(2)}) copy-start(bf16[3,1024,256]{2,1,0:T(8,128)(2,1)S(1)} %collective-permute-done.5.refs_6_) | copy-start | bytes 4718596
  88.3 9.0 %collective-permute-start.6 = (bf16[3,1024,256]{2,1,0:T(8,128)(2,1)S(1)}, bf16[3,1024,256]{2,1,0:T(8,128)(2,1)}, u32[]{:S(2)}, u32[]{:S(2)}) collective-permute-start(bf16[3,1024,256]{2,1,0:T(8,128)(2,1)S(1)} %collective-permute-done.5.refs_6_), channel_id=1, source_target_pairs={{0,1},{1,0},{2,3},{3,2},{4,5},{5,4},{6,7},{7,6},{8,9},{9,8},{10,11... | collective-permute-start | bytes 4718600 | tf_op jit(solution)/shard_map/ppermute | solution.py:198
  94.2 1.1 copy-start.3
  94.2 1.7 %copy-start.4 = (bf16[3,1024,256]{2,1,0:T(8,128)(2,1)}, bf16[3,1024,256]{2,1,0:T(8,128)(2,1)S(1)}, u32[]{:S(2)}) copy-start(bf16[3,1024,256]{2,1,0:T(8,128)(2,1)S(1)} %collective-permute-done.4.refs_5_) | copy-start | bytes 4718596
  95.9 1.1 copy-start.5
  97.3 60.8 %copy-start.6 = (bf16[320,128]{1,0:T(8,128)(2,1)S(1)}, bf16[320,128]{1,0:T(8,128)(2,1)}, u32[]{:S(2)}) copy-start(bf16[320,128]{1,0:T(8,128)(2,1)} %get-tuple-element.8) | copy-start | bytes 245764

commit v6 on v5

--- a/solution.py
+++ b/solution.py
@@ -184,23 +184,20 @@
 
 
 def gather_weights(weights):
-    core = lax.axis_index("tensor") % 2
-    chips = lax.axis_size("tensor") // 2
-
-    def shift(value, step0, step1):
-        pairs = []
-        for chip in range(chips):
-            pairs.append((2 * chip, 2 * ((chip + step0) % chips)))
-            pairs.append((2 * chip + 1, 2 * ((chip + step1) % chips) + 1))
+    count = lax.axis_size("tensor")
+
+    def move(value, pairs):
         return lax.ppermute(value, "tensor", pairs)
 
-    def swap(value):
-        return lax.ppermute(value, "tensor", [(i, i ^ 1) for i in range(2 * chips)])
-
-    left = shift(weights, 1, 1)
-    right = shift(weights, -1, -1)
-    far = shift(jnp.where(core == 0, left, right), 1, -1)
-    return [weights, swap(weights), left, right, swap(left), swap(right), far, swap(far)]
+    swap_pairs = [(i, i ^ 1) for i in range(count)]
+    ring_pairs = [(i, (i + 2 - 4 * (i % 2)) % count) for i in range(count)]
+    blocks = []
+    held = weights
+    for hop in range(count // 2):
+        blocks += [held, move(held, swap_pairs)]
+        if hop + 1 < count // 2:
+            held = move(held, ring_pairs)
+    return blocks
 
 
 def on_device(tokens, out_grad, expert_ids, gate_levels, gate_weight, up_weight, down_weight):

time: 161 us -> 151 us (0.938)
  waiting for transfers between devices: 47.8 us -> 26.2 us
  starting transfers between devices: 41.8 us -> 56.8 us
  blocking collectives: 49.7 us -> 45.3 us
    ppermute x7, waiting for transfers between devices: 47.8 us -> 23.2 us  [move(): return lax.ppermute(value, 'tensor', pairs)]
    ppermute x7, starting transfers between devices: 22.3 us -> 38.3 us  [move(): return lax.ppermute(value, 'tensor', pairs)]
    all_to_all x1, blocking collectives: 49.7 us -> 45.3 us  [on_device(): lax.all_to_all(result, 'expert', split_axis=0, concat_axis=0, tiled=True)]
    all_to_all x1, waiting for transfers between devices: 0.01 us -> 2.98 us  [on_device(): lax.all_to_all(send, 'expert', split_axis=0, concat_axis=0, tiled=True)]
    unnamed x14 -> x12, local copies, waits for them, and re-layouts: 2.86 us -> 3.4 us
  transfers between devices with their start and end apart: 8 -> 8, of which waited for: 4 -> 3; matrix products, arithmetic and copies ran while one was open for 0% -> 0% of each run, Pallas kernels for 0% -> 0%
where the time goes in v6:
time: 151 us; the launch traced here: 149 us
  starting transfers between devices  56.8 us (38%)
  blocking collectives  45.3 us (30%)
  waiting for transfers between devices  26.2 us (17%)
  Pallas kernels  15.7 us (10%)
  local copies, waits for them, and re-layouts  3.4 us (2%)
    all_to_all x1, blocking collectives, on_device(): lax.all_to_all(result, 'expert', split_axis=0, concat_axis=0, tiled=True)  45.3 us
    ppermute x7, starting transfers between devices, move(): return lax.ppermute(value, 'tensor', pairs)  38.3 us
    ppermute x7, waiting for transfers between devices, move(): return lax.ppermute(value, 'tensor', pairs)  23.2 us
    all_to_all x1, starting transfers between devices, on_device(): lax.all_to_all(send, 'expert', split_axis=0, concat_axis=0, tiled=True)  18.5 us
    pallas_call x1, Pallas kernels, call_expert(): pl.pallas_call(expert_kernel, name='expert_grad', out_shape=jax.ShapeDtyp...  11.2 us
    pallas_call x1, Pallas kernels, call_route(): pl.pallas_call(lambda *refs: route_kernel(capacity, experts, *refs), name...  4.54 us
    unnamed x12, local copies, waits for them, and re-layouts  3.4 us
  transfers between devices with their start and end apart: 8, of which 3 were waited for; matrix products, arithmetic and copies ran while one was open for 0% of the time, Pallas kernels for 0%

profile of v6, /device:TPU:1, one launch (start us, length us, event | category | flops | bytes accessed | tf_op | source)
XLA Modules:
  0.0 148.5 jit_solution(11407113620968465691)
XLA Ops:
  0.0 4.5 %route.1 = (bf16[5120,128]{1,0:T(8,128)(2,1)}, bf16[320,128]{1,0:T(8,128)(2,1)}, bf16[3,1024,256]{2,1,0:T(8,128)(2,1)}) custom-call(bf16[128,1024]{1,0:T(8,128)(2,1)} %refs_0_.1, bf16[128,1024]{1,0:T(8,128)(2,1)} %refs_1_.1, s32[2,128]{1,0:T(2,128)} %bitcast.14, s32[2,128]{1,0:T(2,128)} %bitcast.15, bf16[1,1024,256]{2,1,0:T(8,128)(2,1)} %refs_4_.1, ...), custom_call_target="tpu_custom_call" | custom-call | tf_op jit(solution)/shard_map/route/pallas_call | solution.py:67
  4.6 0.0 copy-start.1
  4.6 5.3 %collective-permute-start.1 = (bf16[3,1024,256]{2,1,0:T(8,128)(2,1)}, bf16[3,1024,256]{2,1,0:T(8,128)(2,1)}, u32[]{:S(2)}, u32[]{:S(2)}) collective-permute-start(bf16[3,1024,256]{2,1,0:T(8,128)(2,1)} %get-tuple-element.10.refs_0_), channel_id=1, source_target_pairs={{0,2},{1,7},{2,4},{3,1},{4,6},{5,3},{6,0},{7,5},{8,10},{9,15},{10,... | collective-permute-start | bytes 4718600 | tf_op jit(solution)/shard_map/ppermute | solution.py:190
  9.9 18.5 %all-to-all-start = ((bf16[64,80,128]{2,1,0:T(8,128)(2,1)}), bf16[64,80,128]{2,1,0:T(8,128)(2,1)S(1)}, u32[]{:S(2)}, u32[]{:S(2)}) async-start(bf16[64,80,128]{2,1,0:T(8,128)(2,1)} %bitcast.13), calls=%async_computation | async-start | bytes 2621440 | tf_op jit(solution)/shard_map/all_to_all | solution.py:213
  28.4 0.0 collective-permute-done.1.refs_2_
  28.4 4.2 %collective-permute-start.3 = (bf16[3,1024,256]{2,1,0:T(8,128)(2,1)}, bf16[3,1024,256]{2,1,0:T(8,128)(2,1)S(1)}, u32[]{:S(2)}, u32[]{:S(2)}) collective-permute-start(bf16[3,1024,256]{2,1,0:T(8,128)(2,1)} %collective-permute-done.1.refs_2_), channel_id=1, source_target_pairs={{0,2},{1,7},{2,4},{3,1},{4,6},{5,3},{6,0},{7,5},{8,10},{9,15},{10,... | collective-permute-start | bytes 4718600 | tf_op jit(solution)/shard_map/ppermute | solution.py:190
  32.6 17.7 %collective-permute-done.3.refs_4_ = bf16[3,1024,256]{2,1,0:T(8,128)(2,1)S(1)} collective-permute-done((bf16[3,1024,256]{2,1,0:T(8,128)(2,1)}, bf16[3,1024,256]{2,1,0:T(8,128)(2,1)S(1)}, u32[]{:S(2)}, u32[]{:S(2)}) %collective-permute-start.3) | collective-permute-done | bytes 1572896 | tf_op jit(solution)/shard_map/ppermute | solution.py:190
  50.2 0.0 copy-start.2
  50.2 5.2 %collective-permute-start.5 = (bf16[3,1024,256]{2,1,0:T(8,128)(2,1)S(1)}, bf16[3,1024,256]{2,1,0:T(8,128)(2,1)}, u32[]{:S(2)}, u32[]{:S(2)}) collective-permute-start(bf16[3,1024,256]{2,1,0:T(8,128)(2,1)S(1)} %collective-permute-done.3.refs_4_), channel_id=1, source_target_pairs={{0,2},{1,7},{2,4},{3,1},{4,6},{5,3},{6,0},{7,5},{8,10},{9,15},{10,... | collective-permute-start | bytes 4718600 | tf_op jit(solution)/shard_map/ppermute | solution.py:190
  55.4 0.0 copy-done.1
  55.5 7.5 %collective-permute-start = (bf16[3,1024,256]{2,1,0:T(8,128)(2,1)S(1)}, bf16[3,1024,256]{2,1,0:T(8,128)(2,1)S(1)}, u32[]{:S(2)}, u32[]{:S(2)}) collective-permute-start(bf16[3,1024,256]{2,1,0:T(8,128)(2,1)S(1)} %copy-done.1), channel_id=1, source_target_pairs={{0,1},{1,0},{2,3},{3,2},{4,5},{5,4},{6,7},{7,6},{8,9},{9,8},{10,11... | collective-permute-start | bytes 4718600 | tf_op jit(solution)/shard_map/ppermute | solution.py:190
  62.9 1.9 %collective-permute-start.2 = (bf16[3,1024,256]{2,1,0:T(8,128)(2,1)}, bf16[3,1024,256]{2,1,0:T(8,128)(2,1)S(1)}, u32[]{:S(2)}, u32[]{:S(2)}) collective-permute-start(bf16[3,1024,256]{2,1,0:T(8,128)(2,1)} %collective-permute-done.1.refs_2_), channel_id=1, source_target_pairs={{0,1},{1,0},{2,3},{3,2},{4,5},{5,4},{6,7},{7,6},{8,9},{9,8},{10,11... | collective-permute-start | bytes 4718600 | tf_op jit(solution)/shard_map/ppermute | solution.py:190
  64.9 2.4 %collective-permute-start.4 = (bf16[3,1024,256]{2,1,0:T(8,128)(2,1)S(1)}, bf16[3,1024,256]{2,1,0:T(8,128)(2,1)}, u32[]{:S(2)}, u32[]{:S(2)}) collective-permute-start(bf16[3,1024,256]{2,1,0:T(8,128)(2,1)S(1)} %collective-permute-done.3.refs_4_), channel_id=1, source_target_pairs={{0,1},{1,0},{2,3},{3,2},{4,5},{5,4},{6,7},{7,6},{8,9},{9,8},{10,11... | collective-permute-start | bytes 4718600 | tf_op jit(solution)/shard_map/ppermute | solution.py:190
  67.3 5.5 %collective-permute-done.5.refs_6_ = bf16[3,1024,256]{2,1,0:T(8,128)(2,1)} collective-permute-done((bf16[3,1024,256]{2,1,0:T(8,128)(2,1)S(1)}, bf16[3,1024,256]{2,1,0:T(8,128)(2,1)}, u32[]{:S(2)}, u32[]{:S(2)}) %collective-permute-start.5) | collective-permute-done | bytes 1572896 | tf_op jit(solution)/shard_map/ppermute | solution.py:190
  72.8 11.8 %collective-permute-start.6 = (bf16[3,1024,256]{2,1,0:T(8,128)(2,1)}, bf16[3,1024,256]{2,1,0:T(8,128)(2,1)}, u32[]{:S(2)}, u32[]{:S(2)}) collective-permute-start(bf16[3,1024,256]{2,1,0:T(8,128)(2,1)} %collective-permute-done.5.refs_6_), channel_id=1, source_target_pairs={{0,1},{1,0},{2,3},{3,2},{4,5},{5,4},{6,7},{7,6},{8,9},{9,8},{10,11... | collective-permute-start | bytes 4718600 | tf_op jit(solution)/shard_map/ppermute | solution.py:190
  84.6 0.0 collective-permute-done.refs_1_
  84.6 0.0 copy-start.3
  84.6 0.0 collective-permute-done.2.refs_3_
  84.6 0.0 copy-done.2
  84.7 1.1 copy-done.3
  85.8 0.0 copy-start.4
  85.8 1.2 copy-done.4
  86.9 0.0 collective-permute-done.4.refs_5_
  86.9 3.0 %all-to-all-done = bf16[64,80,128]{2,1,0:T(8,128)(2,1)S(1)} async-done(((bf16[64,80,128]{2,1,0:T(8,128)(2,1)}), bf16[64,80,128]{2,1,0:T(8,128)(2,1)S(1)}, u32[]{:S(2)}, u32[]{:S(2)}) %all-to-all-start) | async-done | bytes 1310752 | tf_op jit(solution)/shard_map/all_to_all | solution.py:213
  89.9 0.0 copy-start
  89.9 0.0 collective-permute-done.6.refs_7_
  89.9 1.1 copy-done
  91.0 0.0 copy-start.5
  91.0 11.2 %expert_grad.1 = bf16[2560,128]{1,0:T(8,128)(2,1)} custom-call(bf16[5120,128]{1,0:T(8,128)(2,1)} %bitcast.10, bf16[3,1024,256]{2,1,0:T(8,128)(2,1)} %get-tuple-element.10.refs_0_, bf16[3,1024,256]{2,1,0:T(8,128)(2,1)} %copy-done.3, bf16[3,1024,256]{2,1,0:T(8,128)(2,1)} %collective-permute-done.1.refs_2_, bf16[3,1024,256]{2,1,0:T(8,128)(2,1)} %copy-done.4, ...), custom_call_target="tpu_custom_call" | custom-call | tf_op jit(solution)/shard_map/expert_grad/pallas_call | solution.py:164
  102.2 45.3 %all_to_all.16 = bf16[320,8,128]{2,1,0:T(8,128)(2,1)S(1)} all-to-all(bf16[320,8,128]{2,1,0:T(8,128)(2,1)} %bitcast.11), channel_id=1, replica_groups=mesh['expert'=64,'tensor'=8] {'expert'}, dimensions={0} | all-to-all | bytes 1310720 | tf_op jit(solution)/shard_map/all_to_all | solution.py:217
  147.5 0.0 copy-done.5
  147.5 1.0 convolution_convert_fusion
Async XLA Ops:
  4.6 50.9 %copy-start.1 = (bf16[3,1024,256]{2,1,0:T(8,128)(2,1)S(1)}, bf16[3,1024,256]{2,1,0:T(8,128)(2,1)}, u32[]{:S(2)}) copy-start(bf16[3,1024,256]{2,1,0:T(8,128)(2,1)} %get-tuple-element.10.refs_0_) | copy-start | bytes 4718596
  4.6 23.8 %collective-permute-start.1 = (bf16[3,1024,256]{2,1,0:T(8,128)(2,1)}, bf16[3,1024,256]{2,1,0:T(8,128)(2,1)}, u32[]{:S(2)}, u32[]{:S(2)}) collective-permute-start(bf16[3,1024,256]{2,1,0:T(8,128)(2,1)} %get-tuple-element.10.refs_0_), channel_id=1, source_target_pairs={{0,2},{1,7},{2,4},{3,1},{4,6},{5,3},{6,0},{7,5},{8,10},{9,15},{10,... | collective-permute-start | bytes 4718600 | tf_op jit(solution)/shard_map/ppermute | solution.py:190
  9.9 80.0 %all-to-all-start = ((bf16[64,80,128]{2,1,0:T(8,128)(2,1)}), bf16[64,80,128]{2,1,0:T(8,128)(2,1)S(1)}, u32[]{:S(2)}, u32[]{:S(2)}) async-start(bf16[64,80,128]{2,1,0:T(8,128)(2,1)} %bitcast.13), calls=%async_computation | async-start | bytes 2621440 | tf_op jit(solution)/shard_map/all_to_all | solution.py:213
  28.4 21.9 %collective-permute-start.3 = (bf16[3,1024,256]{2,1,0:T(8,128)(2,1)}, bf16[3,1024,256]{2,1,0:T(8,128)(2,1)S(1)}, u32[]{:S(2)}, u32[]{:S(2)}) collective-permute-start(bf16[3,1024,256]{2,1,0:T(8,128)(2,1)} %collective-permute-done.1.refs_2_), channel_id=1, source_target_pairs={{0,2},{1,7},{2,4},{3,1},{4,6},{5,3},{6,0},{7,5},{8,10},{9,15},{10,... | collective-permute-start | bytes 4718600 | tf_op jit(solution)/shard_map/ppermute | solution.py:190
  50.2 34.4 %copy-start.2 = (bf16[3,1024,256]{2,1,0:T(8,128)(2,1)}, bf16[3,1024,256]{2,1,0:T(8,128)(2,1)S(1)}, u32[]{:S(2)}) copy-start(bf16[3,1024,256]{2,1,0:T(8,128)(2,1)S(1)} %collective-permute-done.3.refs_4_) | copy-start | bytes 4718596
  50.2 22.6 %collective-permute-start.5 = (bf16[3,1024,256]{2,1,0:T(8,128)(2,1)S(1)}, bf16[3,1024,256]{2,1,0:T(8,128)(2,1)}, u32[]{:S(2)}, u32[]{:S(2)}) collective-permute-start(bf16[3,1024,256]{2,1,0:T(8,128)(2,1)S(1)} %collective-permute-done.3.refs_4_), channel_id=1, source_target_pairs={{0,2},{1,7},{2,4},{3,1},{4,6},{5,3},{6,0},{7,5},{8,10},{9,15},{10,... | collective-permute-start | bytes 4718600 | tf_op jit(solution)/shard_map/ppermute | solution.py:190
  55.5 29.2 %collective-permute-start = (bf16[3,1024,256]{2,1,0:T(8,128)(2,1)S(1)}, bf16[3,1024,256]{2,1,0:T(8,128)(2,1)S(1)}, u32[]{:S(2)}, u32[]{:S(2)}) collective-permute-start(bf16[3,1024,256]{2,1,0:T(8,128)(2,1)S(1)} %copy-done.1), channel_id=1, source_target_pairs={{0,1},{1,0},{2,3},{3,2},{4,5},{5,4},{6,7},{7,6},{8,9},{9,8},{10,11... | collective-permute-start | bytes 4718600 | tf_op jit(solution)/shard_map/ppermute | solution.py:190
  62.9 21.7 %collective-permute-start.2 = (bf16[3,1024,256]{2,1,0:T(8,128)(2,1)}, bf16[3,1024,256]{2,1,0:T(8,128)(2,1)S(1)}, u32[]{:S(2)}, u32[]{:S(2)}) collective-permute-start(bf16[3,1024,256]{2,1,0:T(8,128)(2,1)} %collective-permute-done.1.refs_2_), channel_id=1, source_target_pairs={{0,1},{1,0},{2,3},{3,2},{4,5},{5,4},{6,7},{7,6},{8,9},{9,8},{10,11... | collective-permute-start | bytes 4718600 | tf_op jit(solution)/shard_map/ppermute | solution.py:190
  64.9 22.1 %collective-permute-start.4 = (bf16[3,1024,256]{2,1,0:T(8,128)(2,1)S(1)}, bf16[3,1024,256]{2,1,0:T(8,128)(2,1)}, u32[]{:S(2)}, u32[]{:S(2)}) collective-permute-start(bf16[3,1024,256]{2,1,0:T(8,128)(2,1)S(1)} %collective-permute-done.3.refs_4_), channel_id=1, source_target_pairs={{0,1},{1,0},{2,3},{3,2},{4,5},{5,4},{6,7},{7,6},{8,9},{9,8},{10,11... | collective-permute-start | bytes 4718600 | tf_op jit(solution)/shard_map/ppermute | solution.py:190
  72.8 17.1 %collective-permute-start.6 = (bf16[3,1024,256]{2,1,0:T(8,128)(2,1)}, bf16[3,1024,256]{2,1,0:T(8,128)(2,1)}, u32[]{:S(2)}, u32[]{:S(2)}) collective-permute-start(bf16[3,1024,256]{2,1,0:T(8,128)(2,1)} %collective-permute-done.5.refs_6_), channel_id=1, source_target_pairs={{0,1},{1,0},{2,3},{3,2},{4,5},{5,4},{6,7},{7,6},{8,9},{9,8},{10,11... | collective-permute-start | bytes 4718600 | tf_op jit(solution)/shard_map/ppermute | solution.py:190
  84.6 1.1 copy-start.3
  85.8 1.2 copy-start.4
  89.9 1.1 copy-start
  91.0 56.5 %copy-start.5 = (bf16[320,128]{1,0:T(8,128)(2,1)S(1)}, bf16[320,128]{1,0:T(8,128)(2,1)}, u32[]{:S(2)}) copy-start(bf16[320,128]{1,0:T(8,128)(2,1)} %get-tuple-element.8) | copy-start | bytes 245764

commit v7 on v6

--- a/solution.py
+++ b/solution.py
@@ -179,7 +179,7 @@
             pltpu.SemaphoreType.DMA((chunks,)),
             pltpu.SemaphoreType.DMA((chunks,)),
         ],
-        compiler_params=pltpu.CompilerParams(vmem_limit_bytes=vmem_limit),
+        compiler_params=pltpu.CompilerParams(vmem_limit_bytes=52 * 1024 * 1024),
     )(rows, *blocks)
 
 
@@ -191,12 +191,13 @@
 
     swap_pairs = [(i, i ^ 1) for i in range(count)]
     ring_pairs = [(i, (i + 2 - 4 * (i % 2)) % count) for i in range(count)]
+    back_pairs = [(i, (i - 2 + 4 * (i % 2)) % count) for i in range(count)]
+    near = move(weights, ring_pairs)
+    other = move(weights, back_pairs)
+    far = move(near, ring_pairs)
     blocks = []
-    held = weights
-    for hop in range(count // 2):
+    for held in (weights, near, other, far):
         blocks += [held, move(held, swap_pairs)]
-        if hop + 1 < count // 2:
-            held = move(held, ring_pairs)
     return blocks
 
 

time: 151 us -> 156 us (1.033)
  waiting for transfers between devices: 26.2 us -> 38 us
  starting transfers between devices: 56.8 us -> 45.5 us
  blocking collectives: 45.3 us -> 50.1 us
    ppermute x7, waiting for transfers between devices: 23.2 us -> 38 us  [move(): return lax.ppermute(value, 'tensor', pairs)]
    ppermute x7, starting transfers between devices: 38.3 us -> 26.1 us  [move(): return lax.ppermute(value, 'tensor', pairs)]
    all_to_all x1, blocking collectives: 45.3 us -> 50.1 us  [on_device(): lax.all_to_all(result, 'expert', split_axis=0, concat_axis=0, tiled=True)]
    all_to_all x1, waiting for transfers between devices: 2.98 us -> 0.01 us  [on_device(): lax.all_to_all(send, 'expert', split_axis=0, concat_axis=0, tiled=True)]
    unnamed x12 -> x16, local copies, waits for them, and re-layouts: 3.4 us -> 2.88 us
where the time goes in v7:
time: 156 us; the launch traced here: 153 us
  blocking collectives  50.1 us (32%)
  starting transfers between devices  45.5 us (29%)
  waiting for transfers between devices  38 us (24%)
  Pallas kernels  15.7 us (10%)
  local copies, waits for them, and re-layouts  2.88 us (2%)
    all_to_all x1, blocking collectives, on_device(): lax.all_to_all(result, 'expert', split_axis=0, concat_axis=0, tiled=True)  50.1 us
    ppermute x7, waiting for transfers between devices, move(): return lax.ppermute(value, 'tensor', pairs)  38 us
    ppermute x7, starting transfers between devices, move(): return lax.ppermute(value, 'tensor', pairs)  26.1 us
    all_to_all x1, starting transfers between devices, on_device(): lax.all_to_all(send, 'expert', split_axis=0, concat_axis=0, tiled=True)  19.4 us
    pallas_call x1, Pallas kernels, call_expert(): pl.pallas_call(expert_kernel, name='expert_grad', out_shape=jax.ShapeDtyp...  11.2 us
    pallas_call x1, Pallas kernels, call_route(): pl.pallas_call(lambda *refs: route_kernel(capacity, experts, *refs), name...  4.55 us
  transfers between devices with their start and end apart: 8, of which 3 were waited for; matrix products, arithmetic and copies ran while one was open for 0% of the time, Pallas kernels for 0%

profile of v7, /device:TPU:1, one launch (start us, length us, event | category | flops | bytes accessed | tf_op | source)
XLA Modules:
  0.0 153.5 jit_solution(3608296035391176783)
XLA Ops:
  0.0 4.5 %route.1 = (bf16[5120,128]{1,0:T(8,128)(2,1)}, bf16[320,128]{1,0:T(8,128)(2,1)}, bf16[3,1024,256]{2,1,0:T(8,128)(2,1)}) custom-call(bf16[128,1024]{1,0:T(8,128)(2,1)} %refs_0_.1, bf16[128,1024]{1,0:T(8,128)(2,1)} %refs_1_.1, s32[2,128]{1,0:T(2,128)} %bitcast.14, s32[2,128]{1,0:T(2,128)} %bitcast.15, bf16[1,1024,256]{2,1,0:T(8,128)(2,1)} %refs_4_.1, ...), custom_call_target="tpu_custom_call" | custom-call | tf_op jit(solution)/shard_map/route/pallas_call | solution.py:67
  4.6 0.0 copy-start
  4.6 19.4 %all-to-all-start = ((bf16[64,80,128]{2,1,0:T(8,128)(2,1)}), bf16[64,80,128]{2,1,0:T(8,128)(2,1)S(1)}, u32[]{:S(2)}, u32[]{:S(2)}) async-start(bf16[64,80,128]{2,1,0:T(8,128)(2,1)} %bitcast.13), calls=%async_computation | async-start | bytes 2621440 | tf_op jit(solution)/shard_map/all_to_all | solution.py:214
  24.0 0.0 copy-done
  24.0 4.4 %collective-permute-start.1 = (bf16[3,1024,256]{2,1,0:T(8,128)(2,1)S(1)}, bf16[3,1024,256]{2,1,0:T(8,128)(2,1)S(1)}, u32[]{:S(2)}, u32[]{:S(2)}) collective-permute-start(bf16[3,1024,256]{2,1,0:T(8,128)(2,1)S(1)} %copy-done), channel_id=1, source_target_pairs={{0,2},{1,7},{2,4},{3,1},{4,6},{5,3},{6,0},{7,5},{8,10},{9,15},{10,... | collective-permute-start | bytes 4718600 | tf_op jit(solution)/shard_map/ppermute | solution.py:190
  28.4 1.9 %collective-permute-start.3 = (bf16[3,1024,256]{2,1,0:T(8,128)(2,1)S(1)}, bf16[3,1024,256]{2,1,0:T(8,128)(2,1)S(1)}, u32[]{:S(2)}, u32[]{:S(2)}) collective-permute-start(bf16[3,1024,256]{2,1,0:T(8,128)(2,1)S(1)} %copy-done), channel_id=1, source_target_pairs={{0,6},{1,3},{2,0},{3,5},{4,2},{5,7},{6,4},{7,1},{8,14},{9,11},{10,... | collective-permute-start | bytes 4718600 | tf_op jit(solution)/shard_map/ppermute | solution.py:190
  30.3 28.4 %collective-permute-done.1.refs_2_ = bf16[3,1024,256]{2,1,0:T(8,128)(2,1)S(1)} collective-permute-done((bf16[3,1024,256]{2,1,0:T(8,128)(2,1)S(1)}, bf16[3,1024,256]{2,1,0:T(8,128)(2,1)S(1)}, u32[]{:S(2)}, u32[]{:S(2)}) %collective-permute-start.1) | collective-permute-done | bytes 1572896 | tf_op jit(solution)/shard_map/ppermute | solution.py:190
  58.8 0.0 copy-start.1
  58.8 5.3 %collective-permute-start.5 = (bf16[3,1024,256]{2,1,0:T(8,128)(2,1)S(1)}, bf16[3,1024,256]{2,1,0:T(8,128)(2,1)S(1)}, u32[]{:S(2)}, u32[]{:S(2)}) collective-permute-start(bf16[3,1024,256]{2,1,0:T(8,128)(2,1)S(1)} %collective-permute-done.1.refs_2_), channel_id=1, source_target_pairs={{0,2},{1,7},{2,4},{3,1},{4,6},{5,3},{6,0},{7,5},{8,10},{9,15},{10,... | collective-permute-start | bytes 4718600 | tf_op jit(solution)/shard_map/ppermute | solution.py:190
  64.1 3.6 %collective-permute-start = (bf16[3,1024,256]{2,1,0:T(8,128)(2,1)S(1)}, bf16[3,1024,256]{2,1,0:T(8,128)(2,1)S(1)}, u32[]{:S(2)}, u32[]{:S(2)}) collective-permute-start(bf16[3,1024,256]{2,1,0:T(8,128)(2,1)S(1)} %copy-done), channel_id=1, source_target_pairs={{0,1},{1,0},{2,3},{3,2},{4,5},{5,4},{6,7},{7,6},{8,9},{9,8},{10,11... | collective-permute-start | bytes 4718600 | tf_op jit(solution)/shard_map/ppermute | solution.py:190
  67.7 1.9 %collective-permute-start.2 = (bf16[3,1024,256]{2,1,0:T(8,128)(2,1)S(1)}, bf16[3,1024,256]{2,1,0:T(8,128)(2,1)S(1)}, u32[]{:S(2)}, u32[]{:S(2)}) collective-permute-start(bf16[3,1024,256]{2,1,0:T(8,128)(2,1)S(1)} %collective-permute-done.1.refs_2_), channel_id=1, source_target_pairs={{0,1},{1,0},{2,3},{3,2},{4,5},{5,4},{6,7},{7,6},{8,9},{9,8},{10,11... | collective-permute-start | bytes 4718600 | tf_op jit(solution)/shard_map/ppermute | solution.py:190
  69.6 0.0 collective-permute-done.3.refs_4_
  69.6 0.0 copy-start.2
  69.6 2.4 %collective-permute-start.4 = (bf16[3,1024,256]{2,1,0:T(8,128)(2,1)S(1)}, bf16[3,1024,256]{2,1,0:T(8,128)(2,1)S(1)}, u32[]{:S(2)}, u32[]{:S(2)}) collective-permute-start(bf16[3,1024,256]{2,1,0:T(8,128)(2,1)S(1)} %collective-permute-done.3.refs_4_), channel_id=1, source_target_pairs={{0,1},{1,0},{2,3},{3,2},{4,5},{5,4},{6,7},{7,6},{8,9},{9,8},{10,11... | collective-permute-start | bytes 4718600 | tf_op jit(solution)/shard_map/ppermute | solution.py:190
  72.0 9.4 %collective-permute-done.5.refs_6_ = bf16[3,1024,256]{2,1,0:T(8,128)(2,1)S(1)} collective-permute-done((bf16[3,1024,256]{2,1,0:T(8,128)(2,1)S(1)}, bf16[3,1024,256]{2,1,0:T(8,128)(2,1)S(1)}, u32[]{:S(2)}, u32[]{:S(2)}) %collective-permute-start.5) | collective-permute-done | bytes 1572896 | tf_op jit(solution)/shard_map/ppermute | solution.py:190
  81.4 0.0 copy-start.3
  81.4 6.6 %collective-permute-start.6 = (bf16[3,1024,256]{2,1,0:T(8,128)(2,1)S(1)}, bf16[3,1024,256]{2,1,0:T(8,128)(2,1)}, u32[]{:S(2)}, u32[]{:S(2)}) collective-permute-start(bf16[3,1024,256]{2,1,0:T(8,128)(2,1)S(1)} %collective-permute-done.5.refs_6_), channel_id=1, source_target_pairs={{0,1},{1,0},{2,3},{3,2},{4,5},{5,4},{6,7},{7,6},{8,9},{9,8},{10,11... | collective-permute-start | bytes 4718600 | tf_op jit(solution)/shard_map/ppermute | solution.py:190
  88.0 0.0 collective-permute-done.refs_1_
  88.0 0.0 copy-start.4
  88.0 0.0 collective-permute-done.4.refs_5_
  88.1 0.0 copy-start.6
  88.1 0.0 collective-permute-done.2.refs_3_
  88.1 0.0 copy-done.1
  88.1 0.0 copy-done.2
  88.1 0.0 copy-done.3
  88.1 1.1 copy-done.4
  89.2 0.6 copy-done.6
  89.8 0.0 copy-start.5
  89.8 1.2 copy-done.5
  91.0 0.2 collective-permute-done.6.refs_7_
  91.2 0.0 all-to-all-done
  91.2 0.0 copy-start.7
  91.2 11.2 %expert_grad.1 = bf16[2560,128]{1,0:T(8,128)(2,1)S(1)} custom-call(bf16[5120,128]{1,0:T(8,128)(2,1)S(1)} %bitcast.10, bf16[3,1024,256]{2,1,0:T(8,128)(2,1)} %get-tuple-element.10.refs_0_, bf16[3,1024,256]{2,1,0:T(8,128)(2,1)} %copy-done.4, bf16[3,1024,256]{2,1,0:T(8,128)(2,1)} %copy-done.1, bf16[3,1024,256]{2,1,0:T(8,128)(2,1)} %copy-done.5, ...), custom_call_target="tpu_custom_call" | custom-call | tf_op jit(solution)/shard_map/expert_grad/pallas_call | solution.py:164
  102.4 50.1 %all_to_all.16 = bf16[320,8,128]{2,1,0:T(8,128)(2,1)S(1)} all-to-all(bf16[320,8,128]{2,1,0:T(8,128)(2,1)S(1)} %bitcast.11), channel_id=1, replica_groups=mesh['expert'=64,'tensor'=8] {'expert'}, dimensions={0} | all-to-all | bytes 1310720 | tf_op jit(solution)/shard_map/all_to_all | solution.py:218
  152.4 0.0 copy-done.7
  152.4 1.0 convolution_convert_fusion
Async XLA Ops:
  4.6 19.4 %copy-start = (bf16[3,1024,256]{2,1,0:T(8,128)(2,1)S(1)}, bf16[3,1024,256]{2,1,0:T(8,128)(2,1)}, u32[]{:S(2)}) copy-start(bf16[3,1024,256]{2,1,0:T(8,128)(2,1)} %get-tuple-element.10.refs_0_) | copy-start | bytes 4718596
  4.6 86.6 %all-to-all-start = ((bf16[64,80,128]{2,1,0:T(8,128)(2,1)}), bf16[64,80,128]{2,1,0:T(8,128)(2,1)S(1)}, u32[]{:S(2)}, u32[]{:S(2)}) async-start(bf16[64,80,128]{2,1,0:T(8,128)(2,1)} %bitcast.13), calls=%async_computation | async-start | bytes 2621440 | tf_op jit(solution)/shard_map/all_to_all | solution.py:214
  24.0 34.8 %collective-permute-start.1 = (bf16[3,1024,256]{2,1,0:T(8,128)(2,1)S(1)}, bf16[3,1024,256]{2,1,0:T(8,128)(2,1)S(1)}, u32[]{:S(2)}, u32[]{:S(2)}) collective-permute-start(bf16[3,1024,256]{2,1,0:T(8,128)(2,1)S(1)} %copy-done), channel_id=1, source_target_pairs={{0,2},{1,7},{2,4},{3,1},{4,6},{5,3},{6,0},{7,5},{8,10},{9,15},{10,... | collective-permute-start | bytes 4718600 | tf_op jit(solution)/shard_map/ppermute | solution.py:190
  28.4 41.2 %collective-permute-start.3 = (bf16[3,1024,256]{2,1,0:T(8,128)(2,1)S(1)}, bf16[3,1024,256]{2,1,0:T(8,128)(2,1)S(1)}, u32[]{:S(2)}, u32[]{:S(2)}) collective-permute-start(bf16[3,1024,256]{2,1,0:T(8,128)(2,1)S(1)} %copy-done), channel_id=1, source_target_pairs={{0,6},{1,3},{2,0},{3,5},{4,2},{5,7},{6,4},{7,1},{8,14},{9,11},{10,... | collective-permute-start | bytes 4718600 | tf_op jit(solution)/shard_map/ppermute | solution.py:190
  58.8 29.3 %copy-start.1 = (bf16[3,1024,256]{2,1,0:T(8,128)(2,1)}, bf16[3,1024,256]{2,1,0:T(8,128)(2,1)S(1)}, u32[]{:S(2)}) copy-start(bf16[3,1024,256]{2,1,0:T(8,128)(2,1)S(1)} %collective-permute-done.1.refs_2_) | copy-start | bytes 4718596
  58.8 22.7 %collective-permute-start.5 = (bf16[3,1024,256]{2,1,0:T(8,128)(2,1)S(1)}, bf16[3,1024,256]{2,1,0:T(8,128)(2,1)S(1)}, u32[]{:S(2)}, u32[]{:S(2)}) collective-permute-start(bf16[3,1024,256]{2,1,0:T(8,128)(2,1)S(1)} %collective-permute-done.1.refs_2_), channel_id=1, source_target_pairs={{0,2},{1,7},{2,4},{3,1},{4,6},{5,3},{6,0},{7,5},{8,10},{9,15},{10,... | collective-permute-start | bytes 4718600 | tf_op jit(solution)/shard_map/ppermute | solution.py:190
  64.1 23.9 %collective-permute-start = (bf16[3,1024,256]{2,1,0:T(8,128)(2,1)S(1)}, bf16[3,1024,256]{2,1,0:T(8,128)(2,1)S(1)}, u32[]{:S(2)}, u32[]{:S(2)}) collective-permute-start(bf16[3,1024,256]{2,1,0:T(8,128)(2,1)S(1)} %copy-done), channel_id=1, source_target_pairs={{0,1},{1,0},{2,3},{3,2},{4,5},{5,4},{6,7},{7,6},{8,9},{9,8},{10,11... | collective-permute-start | bytes 4718600 | tf_op jit(solution)/shard_map/ppermute | solution.py:190
  67.7 20.4 %collective-permute-start.2 = (bf16[3,1024,256]{2,1,0:T(8,128)(2,1)S(1)}, bf16[3,1024,256]{2,1,0:T(8,128)(2,1)S(1)}, u32[]{:S(2)}, u32[]{:S(2)}) collective-permute-start(bf16[3,1024,256]{2,1,0:T(8,128)(2,1)S(1)} %collective-permute-done.1.refs_2_), channel_id=1, source_target_pairs={{0,1},{1,0},{2,3},{3,2},{4,5},{5,4},{6,7},{7,6},{8,9},{9,8},{10,11... | collective-permute-start | bytes 4718600 | tf_op jit(solution)/shard_map/ppermute | solution.py:190
  69.6 18.5 %copy-start.2 = (bf16[3,1024,256]{2,1,0:T(8,128)(2,1)}, bf16[3,1024,256]{2,1,0:T(8,128)(2,1)S(1)}, u32[]{:S(2)}) copy-start(bf16[3,1024,256]{2,1,0:T(8,128)(2,1)S(1)} %collective-permute-done.3.refs_4_) | copy-start | bytes 4718596
  69.6 18.4 %collective-permute-start.4 = (bf16[3,1024,256]{2,1,0:T(8,128)(2,1)S(1)}, bf16[3,1024,256]{2,1,0:T(8,128)(2,1)S(1)}, u32[]{:S(2)}, u32[]{:S(2)}) collective-permute-start(bf16[3,1024,256]{2,1,0:T(8,128)(2,1)S(1)} %collective-permute-done.3.refs_4_), channel_id=1, source_target_pairs={{0,1},{1,0},{2,3},{3,2},{4,5},{5,4},{6,7},{7,6},{8,9},{9,8},{10,11... | collective-permute-start | bytes 4718600 | tf_op jit(solution)/shard_map/ppermute | solution.py:190
  81.4 6.7 %copy-start.3 = (bf16[3,1024,256]{2,1,0:T(8,128)(2,1)}, bf16[3,1024,256]{2,1,0:T(8,128)(2,1)S(1)}, u32[]{:S(2)}) copy-start(bf16[3,1024,256]{2,1,0:T(8,128)(2,1)S(1)} %collective-permute-done.5.refs_6_) | copy-start | bytes 4718596
  81.4 9.8 %collective-permute-start.6 = (bf16[3,1024,256]{2,1,0:T(8,128)(2,1)S(1)}, bf16[3,1024,256]{2,1,0:T(8,128)(2,1)}, u32[]{:S(2)}, u32[]{:S(2)}) collective-permute-start(bf16[3,1024,256]{2,1,0:T(8,128)(2,1)S(1)} %collective-permute-done.5.refs_6_), channel_id=1, source_target_pairs={{0,1},{1,0},{2,3},{3,2},{4,5},{5,4},{6,7},{7,6},{8,9},{9,8},{10,11... | collective-permute-start | bytes 4718600 | tf_op jit(solution)/shard_map/ppermute | solution.py:190
  88.0 1.1 copy-start.4
  88.1 1.7 %copy-start.6 = (bf16[3,1024,256]{2,1,0:T(8,128)(2,1)}, bf16[3,1024,256]{2,1,0:T(8,128)(2,1)S(1)}, u32[]{:S(2)}) copy-start(bf16[3,1024,256]{2,1,0:T(8,128)(2,1)S(1)} %collective-permute-done.4.refs_5_) | copy-start | bytes 4718596
  89.8 1.2 copy-start.5
  91.2 61.3 %copy-start.7 = (bf16[320,128]{1,0:T(8,128)(2,1)S(1)}, bf16[320,128]{1,0:T(8,128)(2,1)}, u32[]{:S(2)}) copy-start(bf16[320,128]{1,0:T(8,128)(2,1)} %get-tuple-element.8) | copy-start | bytes 245764

commit v8 on v7

--- a/solution.py
+++ b/solution.py
@@ -83,10 +83,10 @@
     )(tokens, out_grad, ids, levels, *weights)
 
 
-def expert_kernel(rows_hbm, *refs):
-    count = len(refs) - 11
+def expert_kernel(rows_ref, *refs):
+    count = len(refs) - 9
     weights = refs[:count]
-    out_hbm, acc_ref, buf_ref, rows_ref, stage_ref, tok_ref, grad_ref, out_ref, sems, in_sems, out_sems = refs[count:]
+    out_hbm, acc_ref, buf_ref, stage_ref, tok_ref, grad_ref, out_ref, sems, out_sems = refs[count:]
     slots = acc_ref.shape[0]
     rows_per = slots // chunks
     tall = rows_per * 2 * groups
@@ -95,17 +95,11 @@
     def fetch(block):
         return [pltpu.make_async_copy(weights[block].at[i], buf_ref.at[block, i], sems.at[block, i]) for i in range(3)]
 
-    arrivals = []
-    for q in range(chunks):
-        part = pl.ds(q * tall, tall)
-        arrivals.append(pltpu.make_async_copy(rows_hbm.at[part], rows_ref.at[part], in_sems.at[q]))
-        arrivals[-1].start()
     copies = [fetch(block) for block in range(count)]
     for block in range(pair):
         for copy in copies[block]:
             copy.start()
     for q in range(chunks):
-        arrivals[q].wait()
         part = pl.ds(q * tall, tall)
         stage_ref[part, :] = rows_ref[part, :].astype(jnp.float32)
         for half, target in enumerate((tok_ref, grad_ref)):
@@ -165,18 +159,16 @@
         expert_kernel,
         name="expert_grad",
         out_shape=jax.ShapeDtypeStruct(short, jnp.bfloat16),
-        in_specs=[hbm] * (1 + len(blocks)),
+        in_specs=[pl.BlockSpec(memory_space=pltpu.VMEM)] + [hbm] * len(blocks),
         out_specs=hbm,
         scratch_shapes=[
             pltpu.VMEM((slots, width), jnp.float32),
             pltpu.VMEM((len(blocks),) + blocks[0].shape, jnp.bfloat16),
-            pltpu.VMEM((tall, lanes), jnp.bfloat16),
             pltpu.VMEM((tall, lanes), jnp.float32),
             pltpu.VMEM((slots, width), jnp.bfloat16),
             pltpu.VMEM((slots, width), jnp.bfloat16),
             pltpu.VMEM(short, jnp.bfloat16),
             pltpu.SemaphoreType.DMA((len(blocks), 3)),
-            pltpu.SemaphoreType.DMA((chunks,)),
             pltpu.SemaphoreType.DMA((chunks,)),
         ],
         compiler_params=pltpu.CompilerParams(vmem_limit_bytes=52 * 1024 * 1024),

time: 156 us -> 155 us (level)
  no operation moved by 1% of the time
where the time goes in v8:
time: 155 us; the launch traced here: 153 us
  blocking collectives  50.1 us (32%)
  starting transfers between devices  45.5 us (29%)
  waiting for transfers between devices  38 us (25%)
  Pallas kernels  15.3 us (10%)
  local copies, waits for them, and re-layouts  2.88 us (2%)
    all_to_all x1, blocking collectives, on_device(): lax.all_to_all(result, 'expert', split_axis=0, concat_axis=0, tiled=True)  50.1 us
    ppermute x7, waiting for transfers between devices, move(): return lax.ppermute(value, 'tensor', pairs)  38 us
    ppermute x7, starting transfers between devices, move(): return lax.ppermute(value, 'tensor', pairs)  26.1 us
    all_to_all x1, starting transfers between devices, on_device(): lax.all_to_all(send, 'expert', split_axis=0, concat_axis=0, tiled=True)  19.4 us
    pallas_call x1, Pallas kernels, call_expert(): pl.pallas_call(expert_kernel, name='expert_grad', out_shape=jax.ShapeDtyp...  10.8 us
    pallas_call x1, Pallas kernels, call_route(): pl.pallas_call(lambda *refs: route_kernel(capacity, experts, *refs), name...  4.55 us
  transfers between devices with their start and end apart: 8, of which 3 were waited for; matrix products, arithmetic and copies ran while one was open for 0% of the time, Pallas kernels for 0%

profile of v8, /device:TPU:1, one launch (start us, length us, event | category | flops | bytes accessed | tf_op | source)
XLA Modules:
  0.0 153.1 jit_solution(10537885816678980248)
XLA Ops:
  0.0 4.5 %route.1 = (bf16[5120,128]{1,0:T(8,128)(2,1)}, bf16[320,128]{1,0:T(8,128)(2,1)}, bf16[3,1024,256]{2,1,0:T(8,128)(2,1)}) custom-call(bf16[128,1024]{1,0:T(8,128)(2,1)} %refs_0_.1, bf16[128,1024]{1,0:T(8,128)(2,1)} %refs_1_.1, s32[2,128]{1,0:T(2,128)} %bitcast.14, s32[2,128]{1,0:T(2,128)} %bitcast.15, bf16[1,1024,256]{2,1,0:T(8,128)(2,1)} %refs_4_.1, ...), custom_call_target="tpu_custom_call" | custom-call | tf_op jit(solution)/shard_map/route/pallas_call | solution.py:67
  4.6 0.0 copy-start
  4.6 19.4 %all-to-all-start = ((bf16[64,80,128]{2,1,0:T(8,128)(2,1)}), bf16[64,80,128]{2,1,0:T(8,128)(2,1)S(1)}, u32[]{:S(2)}, u32[]{:S(2)}) async-start(bf16[64,80,128]{2,1,0:T(8,128)(2,1)} %bitcast.13), calls=%async_computation | async-start | bytes 2621440 | tf_op jit(solution)/shard_map/all_to_all | solution.py:206
  24.0 0.0 copy-done
  24.0 4.4 %collective-permute-start.1 = (bf16[3,1024,256]{2,1,0:T(8,128)(2,1)S(1)}, bf16[3,1024,256]{2,1,0:T(8,128)(2,1)S(1)}, u32[]{:S(2)}, u32[]{:S(2)}) collective-permute-start(bf16[3,1024,256]{2,1,0:T(8,128)(2,1)S(1)} %copy-done), channel_id=1, source_target_pairs={{0,2},{1,7},{2,4},{3,1},{4,6},{5,3},{6,0},{7,5},{8,10},{9,15},{10,... | collective-permute-start | bytes 4718600 | tf_op jit(solution)/shard_map/ppermute | solution.py:182
  28.4 1.9 %collective-permute-start.3 = (bf16[3,1024,256]{2,1,0:T(8,128)(2,1)S(1)}, bf16[3,1024,256]{2,1,0:T(8,128)(2,1)S(1)}, u32[]{:S(2)}, u32[]{:S(2)}) collective-permute-start(bf16[3,1024,256]{2,1,0:T(8,128)(2,1)S(1)} %copy-done), channel_id=1, source_target_pairs={{0,6},{1,3},{2,0},{3,5},{4,2},{5,7},{6,4},{7,1},{8,14},{9,11},{10,... | collective-permute-start | bytes 4718600 | tf_op jit(solution)/shard_map/ppermute | solution.py:182
  30.3 28.4 %collective-permute-done.1.refs_2_ = bf16[3,1024,256]{2,1,0:T(8,128)(2,1)S(1)} collective-permute-done((bf16[3,1024,256]{2,1,0:T(8,128)(2,1)S(1)}, bf16[3,1024,256]{2,1,0:T(8,128)(2,1)S(1)}, u32[]{:S(2)}, u32[]{:S(2)}) %collective-permute-start.1) | collective-permute-done | bytes 1572896 | tf_op jit(solution)/shard_map/ppermute | solution.py:182
  58.8 0.0 copy-start.1
  58.8 5.3 %collective-permute-start.5 = (bf16[3,1024,256]{2,1,0:T(8,128)(2,1)S(1)}, bf16[3,1024,256]{2,1,0:T(8,128)(2,1)S(1)}, u32[]{:S(2)}, u32[]{:S(2)}) collective-permute-start(bf16[3,1024,256]{2,1,0:T(8,128)(2,1)S(1)} %collective-permute-done.1.refs_2_), channel_id=1, source_target_pairs={{0,2},{1,7},{2,4},{3,1},{4,6},{5,3},{6,0},{7,5},{8,10},{9,15},{10,... | collective-permute-start | bytes 4718600 | tf_op jit(solution)/shard_map/ppermute | solution.py:182
  64.1 3.6 %collective-permute-start = (bf16[3,1024,256]{2,1,0:T(8,128)(2,1)S(1)}, bf16[3,1024,256]{2,1,0:T(8,128)(2,1)S(1)}, u32[]{:S(2)}, u32[]{:S(2)}) collective-permute-start(bf16[3,1024,256]{2,1,0:T(8,128)(2,1)S(1)} %copy-done), channel_id=1, source_target_pairs={{0,1},{1,0},{2,3},{3,2},{4,5},{5,4},{6,7},{7,6},{8,9},{9,8},{10,11... | collective-permute-start | bytes 4718600 | tf_op jit(solution)/shard_map/ppermute | solution.py:182
  67.7 1.9 %collective-permute-start.2 = (bf16[3,1024,256]{2,1,0:T(8,128)(2,1)S(1)}, bf16[3,1024,256]{2,1,0:T(8,128)(2,1)S(1)}, u32[]{:S(2)}, u32[]{:S(2)}) collective-permute-start(bf16[3,1024,256]{2,1,0:T(8,128)(2,1)S(1)} %collective-permute-done.1.refs_2_), channel_id=1, source_target_pairs={{0,1},{1,0},{2,3},{3,2},{4,5},{5,4},{6,7},{7,6},{8,9},{9,8},{10,11... | collective-permute-start | bytes 4718600 | tf_op jit(solution)/shard_map/ppermute | solution.py:182
  69.6 0.0 collective-permute-done.3.refs_4_
  69.6 0.0 copy-start.2
  69.6 2.4 %collective-permute-start.4 = (bf16[3,1024,256]{2,1,0:T(8,128)(2,1)S(1)}, bf16[3,1024,256]{2,1,0:T(8,128)(2,1)S(1)}, u32[]{:S(2)}, u32[]{:S(2)}) collective-permute-start(bf16[3,1024,256]{2,1,0:T(8,128)(2,1)S(1)} %collective-permute-done.3.refs_4_), channel_id=1, source_target_pairs={{0,1},{1,0},{2,3},{3,2},{4,5},{5,4},{6,7},{7,6},{8,9},{9,8},{10,11... | collective-permute-start | bytes 4718600 | tf_op jit(solution)/shard_map/ppermute | solution.py:182
  72.0 9.4 %collective-permute-done.5.refs_6_ = bf16[3,1024,256]{2,1,0:T(8,128)(2,1)S(1)} collective-permute-done((bf16[3,1024,256]{2,1,0:T(8,128)(2,1)S(1)}, bf16[3,1024,256]{2,1,0:T(8,128)(2,1)S(1)}, u32[]{:S(2)}, u32[]{:S(2)}) %collective-permute-start.5) | collective-permute-done | bytes 1572896 | tf_op jit(solution)/shard_map/ppermute | solution.py:182
  81.4 0.0 copy-start.3
  81.4 6.6 %collective-permute-start.6 = (bf16[3,1024,256]{2,1,0:T(8,128)(2,1)S(1)}, bf16[3,1024,256]{2,1,0:T(8,128)(2,1)}, u32[]{:S(2)}, u32[]{:S(2)}) collective-permute-start(bf16[3,1024,256]{2,1,0:T(8,128)(2,1)S(1)} %collective-permute-done.5.refs_6_), channel_id=1, source_target_pairs={{0,1},{1,0},{2,3},{3,2},{4,5},{5,4},{6,7},{7,6},{8,9},{9,8},{10,11... | collective-permute-start | bytes 4718600 | tf_op jit(solution)/shard_map/ppermute | solution.py:182
  88.0 0.0 collective-permute-done.refs_1_
  88.0 0.0 copy-start.4
  88.0 0.0 collective-permute-done.4.refs_5_
  88.1 0.0 copy-start.6
  88.1 0.0 collective-permute-done.2.refs_3_
  88.1 0.0 copy-done.1
  88.1 0.0 copy-done.2
  88.1 0.0 copy-done.3
  88.1 1.1 copy-done.4
  89.2 0.6 copy-done.6
  89.8 0.0 copy-start.5
  89.8 1.2 copy-done.5
  91.0 0.2 collective-permute-done.6.refs_7_
  91.2 0.0 all-to-all-done
  91.2 0.0 copy-start.7
  91.2 10.8 %expert_grad.1 = bf16[2560,128]{1,0:T(8,128)(2,1)S(1)} custom-call(bf16[5120,128]{1,0:T(8,128)(2,1)S(1)} %bitcast.10, bf16[3,1024,256]{2,1,0:T(8,128)(2,1)} %get-tuple-element.10.refs_0_, bf16[3,1024,256]{2,1,0:T(8,128)(2,1)} %copy-done.4, bf16[3,1024,256]{2,1,0:T(8,128)(2,1)} %copy-done.1, bf16[3,1024,256]{2,1,0:T(8,128)(2,1)} %copy-done.5, ...), custom_call_target="tpu_custom_call" | custom-call | tf_op jit(solution)/shard_map/expert_grad/pallas_call | solution.py:158
  102.0 50.1 %all_to_all.16 = bf16[320,8,128]{2,1,0:T(8,128)(2,1)S(1)} all-to-all(bf16[320,8,128]{2,1,0:T(8,128)(2,1)S(1)} %bitcast.11), channel_id=1, replica_groups=mesh['expert'=64,'tensor'=8] {'expert'}, dimensions={0} | all-to-all | bytes 1310720 | tf_op jit(solution)/shard_map/all_to_all | solution.py:210
  152.0 0.0 copy-done.7
  152.0 1.0 convolution_convert_fusion
Async XLA Ops:
  4.6 19.4 %copy-start = (bf16[3,1024,256]{2,1,0:T(8,128)(2,1)S(1)}, bf16[3,1024,256]{2,1,0:T(8,128)(2,1)}, u32[]{:S(2)}) copy-start(bf16[3,1024,256]{2,1,0:T(8,128)(2,1)} %get-tuple-element.10.refs_0_) | copy-start | bytes 4718596
  4.6 86.6 %all-to-all-start = ((bf16[64,80,128]{2,1,0:T(8,128)(2,1)}), bf16[64,80,128]{2,1,0:T(8,128)(2,1)S(1)}, u32[]{:S(2)}, u32[]{:S(2)}) async-start(bf16[64,80,128]{2,1,0:T(8,128)(2,1)} %bitcast.13), calls=%async_computation | async-start | bytes 2621440 | tf_op jit(solution)/shard_map/all_to_all | solution.py:206
  24.0 34.8 %collective-permute-start.1 = (bf16[3,1024,256]{2,1,0:T(8,128)(2,1)S(1)}, bf16[3,1024,256]{2,1,0:T(8,128)(2,1)S(1)}, u32[]{:S(2)}, u32[]{:S(2)}) collective-permute-start(bf16[3,1024,256]{2,1,0:T(8,128)(2,1)S(1)} %copy-done), channel_id=1, source_target_pairs={{0,2},{1,7},{2,4},{3,1},{4,6},{5,3},{6,0},{7,5},{8,10},{9,15},{10,... | collective-permute-start | bytes 4718600 | tf_op jit(solution)/shard_map/ppermute | solution.py:182
  28.4 41.2 %collective-permute-start.3 = (bf16[3,1024,256]{2,1,0:T(8,128)(2,1)S(1)}, bf16[3,1024,256]{2,1,0:T(8,128)(2,1)S(1)}, u32[]{:S(2)}, u32[]{:S(2)}) collective-permute-start(bf16[3,1024,256]{2,1,0:T(8,128)(2,1)S(1)} %copy-done), channel_id=1, source_target_pairs={{0,6},{1,3},{2,0},{3,5},{4,2},{5,7},{6,4},{7,1},{8,14},{9,11},{10,... | collective-permute-start | bytes 4718600 | tf_op jit(solution)/shard_map/ppermute | solution.py:182
  58.8 29.3 %copy-start.1 = (bf16[3,1024,256]{2,1,0:T(8,128)(2,1)}, bf16[3,1024,256]{2,1,0:T(8,128)(2,1)S(1)}, u32[]{:S(2)}) copy-start(bf16[3,1024,256]{2,1,0:T(8,128)(2,1)S(1)} %collective-permute-done.1.refs_2_) | copy-start | bytes 4718596
  58.8 22.7 %collective-permute-start.5 = (bf16[3,1024,256]{2,1,0:T(8,128)(2,1)S(1)}, bf16[3,1024,256]{2,1,0:T(8,128)(2,1)S(1)}, u32[]{:S(2)}, u32[]{:S(2)}) collective-permute-start(bf16[3,1024,256]{2,1,0:T(8,128)(2,1)S(1)} %collective-permute-done.1.refs_2_), channel_id=1, source_target_pairs={{0,2},{1,7},{2,4},{3,1},{4,6},{5,3},{6,0},{7,5},{8,10},{9,15},{10,... | collective-permute-start | bytes 4718600 | tf_op jit(solution)/shard_map/ppermute | solution.py:182
  64.1 23.9 %collective-permute-start = (bf16[3,1024,256]{2,1,0:T(8,128)(2,1)S(1)}, bf16[3,1024,256]{2,1,0:T(8,128)(2,1)S(1)}, u32[]{:S(2)}, u32[]{:S(2)}) collective-permute-start(bf16[3,1024,256]{2,1,0:T(8,128)(2,1)S(1)} %copy-done), channel_id=1, source_target_pairs={{0,1},{1,0},{2,3},{3,2},{4,5},{5,4},{6,7},{7,6},{8,9},{9,8},{10,11... | collective-permute-start | bytes 4718600 | tf_op jit(solution)/shard_map/ppermute | solution.py:182
  67.7 20.4 %collective-permute-start.2 = (bf16[3,1024,256]{2,1,0:T(8,128)(2,1)S(1)}, bf16[3,1024,256]{2,1,0:T(8,128)(2,1)S(1)}, u32[]{:S(2)}, u32[]{:S(2)}) collective-permute-start(bf16[3,1024,256]{2,1,0:T(8,128)(2,1)S(1)} %collective-permute-done.1.refs_2_), channel_id=1, source_target_pairs={{0,1},{1,0},{2,3},{3,2},{4,5},{5,4},{6,7},{7,6},{8,9},{9,8},{10,11... | collective-permute-start | bytes 4718600 | tf_op jit(solution)/shard_map/ppermute | solution.py:182
  69.6 18.5 %copy-start.2 = (bf16[3,1024,256]{2,1,0:T(8,128)(2,1)}, bf16[3,1024,256]{2,1,0:T(8,128)(2,1)S(1)}, u32[]{:S(2)}) copy-start(bf16[3,1024,256]{2,1,0:T(8,128)(2,1)S(1)} %collective-permute-done.3.refs_4_) | copy-start | bytes 4718596
  69.6 18.4 %collective-permute-start.4 = (bf16[3,1024,256]{2,1,0:T(8,128)(2,1)S(1)}, bf16[3,1024,256]{2,1,0:T(8,128)(2,1)S(1)}, u32[]{:S(2)}, u32[]{:S(2)}) collective-permute-start(bf16[3,1024,256]{2,1,0:T(8,128)(2,1)S(1)} %collective-permute-done.3.refs_4_), channel_id=1, source_target_pairs={{0,1},{1,0},{2,3},{3,2},{4,5},{5,4},{6,7},{7,6},{8,9},{9,8},{10,11... | collective-permute-start | bytes 4718600 | tf_op jit(solution)/shard_map/ppermute | solution.py:182
  81.4 6.7 %copy-start.3 = (bf16[3,1024,256]{2,1,0:T(8,128)(2,1)}, bf16[3,1024,256]{2,1,0:T(8,128)(2,1)S(1)}, u32[]{:S(2)}) copy-start(bf16[3,1024,256]{2,1,0:T(8,128)(2,1)S(1)} %collective-permute-done.5.refs_6_) | copy-start | bytes 4718596
  81.4 9.8 %collective-permute-start.6 = (bf16[3,1024,256]{2,1,0:T(8,128)(2,1)S(1)}, bf16[3,1024,256]{2,1,0:T(8,128)(2,1)}, u32[]{:S(2)}, u32[]{:S(2)}) collective-permute-start(bf16[3,1024,256]{2,1,0:T(8,128)(2,1)S(1)} %collective-permute-done.5.refs_6_), channel_id=1, source_target_pairs={{0,1},{1,0},{2,3},{3,2},{4,5},{5,4},{6,7},{7,6},{8,9},{9,8},{10,11... | collective-permute-start | bytes 4718600 | tf_op jit(solution)/shard_map/ppermute | solution.py:182
  88.0 1.1 copy-start.4
  88.1 1.7 %copy-start.6 = (bf16[3,1024,256]{2,1,0:T(8,128)(2,1)}, bf16[3,1024,256]{2,1,0:T(8,128)(2,1)S(1)}, u32[]{:S(2)}) copy-start(bf16[3,1024,256]{2,1,0:T(8,128)(2,1)S(1)} %collective-permute-done.4.refs_5_) | copy-start | bytes 4718596
  89.8 1.2 copy-start.5
  91.2 60.9 %copy-start.7 = (bf16[320,128]{1,0:T(8,128)(2,1)S(1)}, bf16[320,128]{1,0:T(8,128)(2,1)}, u32[]{:S(2)}) copy-start(bf16[320,128]{1,0:T(8,128)(2,1)} %get-tuple-element.8) | copy-start | bytes 245764
